TPU v7x, 128 devices: a whole 4x4x4 slice. The times are simulated.
128 devices in a mesh: seq: 16 (over y, z), batch: 8 (over x, core).
Axes of the slice: x: 4, y: 4, z: 4, core: 2. Of those that a mesh axis runs over, the one named last changes fastest.
Arguments:
- q_nope: bfloat16 [8, 64, 128, 128], P('batch', None, 'seq'), may hold values from -6 to 6
- q_rope: bfloat16 [8, 64, 128, 64], P('batch', None, 'seq'), may hold values from -8 to 8
- absorb_k: bfloat16 [128, 128, 512], P('seq'), may hold values from -0.5 to 0.5
- absorb_v: bfloat16 [128, 512, 128], P('seq'), may hold values from -0.25 to 0.25
- cache_latent: bfloat16 [8, 16384, 512], P('batch', 'seq'), may hold values from -6 to 6
- cache_rope: bfloat16 [8, 16384, 64], P('batch', 'seq'), may hold values from -8 to 8
- draft_latent: bfloat16 [8, 64, 512], P('batch'), may hold values from -6 to 6
- draft_rope: bfloat16 [8, 64, 64], P('batch'), may hold values from -6 to 6
- residual: bfloat16 [512, 7168], P('batch', 'seq'), may hold values from -1.2 to 1.2
- out_proj: bfloat16 [16384, 7168], P('seq'), may hold values from -0.046875 to 0.046875
- norm_gain: float32 [7168], replicated, may hold values from 0.5 to 1.5
- lm_head: bfloat16 [65536, 7168], P(('seq', 'batch')), may hold values from -2.4095235 to 2.4095235
- parent: int32 [8, 64], replicated, may hold values from 0 to 62, as said below
- draft_ids: int32 [8, 64], replicated, may hold values from 0 to 65535
- cache_len: int32 [8], P('batch'), may hold values from 4096 to 16384
- accept_len: int32 [8], P('batch'), may hold values from 1 to 64
Outputs:
- hidden_out: bfloat16 [512, 7168], P('batch', 'seq')
- target_logp: float32 [8, 64], P('batch')
- accepted_score: float32 [8], P('batch')
Inputs may be any that keep to these rules, and one draw needn't show every extreme that they name: parent[b, 0] = 0, and 0 <= parent[b, i] < i for i >= 1.
All inputs are finite; a program needn't handle non-finite values.
Results may differ from a plain program's by a relative error of at most 0.0095.
Values may be sent and summed in bfloat16 or wider, within the bound.
A program may use at most 256 MiB of HBM per device.

v0:
```python
import math

import jax
import jax.numpy as jnp
from jax import lax
from jax.sharding import Mesh
from jax.sharding import PartitionSpec as P

SEQ = ("seq_0", "seq_1")
BATCH = ("batch_0", "batch_1")
SEQ_BATCH = ("seq_0", "seq_1", "batch_0", "batch_1")


masked_value = -1e30
norm_epsilon = 1e-06
highest = lax.Precision.HIGHEST


def sent_together(arrays, axis, dim, along):
    ends, at = ([], 0)
    for a in arrays[:-1]:
        at += a.shape[along]
        ends.append(at)
    both = jnp.concatenate(arrays, axis=along)
    return tuple(jnp.split(lax.all_gather(both, axis, axis=dim, tiled=True), ends, axis=along))


def copy_for_each(array, axis):
    copies = jnp.broadcast_to(array, (lax.axis_size(axis), *array.shape))
    return lax.all_to_all(copies, axis, split_axis=0, concat_axis=0, tiled=True)


def over_copies(array, axis):
    everything = copy_for_each(array, axis)
    return jnp.max(everything, axis=0)


def gathered_once(array, axis):
    leaves = jax.tree.leaves(array)
    sequence = sorted(range(len(leaves)), key=lambda k: -leaves[k].size)
    width = (1, *leaves[sequence[0]].shape)[-1]
    lines = [
        jnp.pad(leaves[k].reshape(-1), (0, -leaves[k].size % width)).reshape(-1, width)
        for k in sequence
    ]
    both, at, found = (lax.all_gather(jnp.concatenate(lines), axis), 0, {})
    for k, line in zip(sequence, lines):
        piece = both[:, at : at + len(line)].reshape(len(both), -1)
        found[k] = piece[:, : leaves[k].size].reshape(-1, *leaves[k].shape)
        at += len(line)
    numbers = iter(range(len(leaves)))
    return jax.tree.map(lambda _: found[next(numbers)], array)


def combined_by_axis(array, axes, combine):
    for axis in axes:
        pieces = gathered_once(array, axis)
        array = jax.tree.map(lambda part: part[0], pieces)
        for k in range(1, lax.axis_size(axis)):
            array = combine(array, jax.tree.map(lambda part: part[k], pieces))
    return array


def ancestry_of(parents):
    draft_count = parents.shape[1]
    indices = jnp.arange(draft_count, dtype=jnp.int32)
    parent_map = (
        (parents[:, :, None] == indices[None, None, :]) & (indices[None, :, None] > 0)
    ).astype(jnp.float32)
    ancestry = jnp.broadcast_to(jnp.eye(draft_count, dtype=jnp.float32), parent_map.shape)
    for doubling in range(draft_count.bit_length() - 1):
        ancestry = ancestry + jnp.einsum("rij,rjk->rik", ancestry, parent_map, precision=highest)
        parent_map = jnp.einsum("rij,rjk->rik", parent_map, parent_map, precision=highest)
    return ancestry > 0.5


def combine_soft(earlier, later):
    top_new = jnp.maximum(earlier[0], later[0])
    mass_new = earlier[1] * jnp.exp(earlier[0] - top_new) + later[1] * jnp.exp(later[0] - top_new)
    return (top_new, mass_new, earlier[2] + later[2])


def body(
    q_nope,
    q_rope,
    absorb_k,
    absorb_v,
    cache_latent,
    cache_rope,
    draft_latent,
    draft_rope,
    residual,
    out_proj,
    norm_gain,
    lm_head,
    parent,
    draft_ids,
    cache_len,
    accept_len,
):
    requests, draft_count, local_heads, nope_width = q_nope.shape
    cache_rows = cache_latent.shape[1]
    score_scale = 1.0 / math.sqrt(nope_width + q_rope.shape[3])
    seq_index = lax.axis_index(SEQ)
    batch_index = lax.axis_index(BATCH)
    query_latent = jnp.einsum(
        "rihn,hnc->rihc", q_nope, absorb_k, preferred_element_type=jnp.float32
    ).astype(jnp.bfloat16)
    query_all, rope_all = sent_together((query_latent, q_rope), SEQ, 2, 3)
    cache_scores = jnp.einsum(
        "rihc,rtc->rhit", query_all, cache_latent, preferred_element_type=jnp.float32
    )
    cache_scores = cache_scores + jnp.einsum(
        "rihe,rte->rhit", rope_all, cache_rope, preferred_element_type=jnp.float32
    )
    positions = seq_index * cache_rows + jnp.arange(cache_rows, dtype=jnp.int32)
    in_cache = positions[None, :] < cache_len[:, None]
    cache_scores = jnp.where(in_cache[:, None, None, :], cache_scores * score_scale, masked_value)
    tree_scores = jnp.einsum(
        "rihc,rjc->rhij", query_all, draft_latent, preferred_element_type=jnp.float32
    )
    tree_scores = tree_scores + jnp.einsum(
        "rihe,rje->rhij", rope_all, draft_rope, preferred_element_type=jnp.float32
    )
    own_parents = lax.dynamic_slice_in_dim(parent, batch_index * requests, requests, 0)
    ancestry = ancestry_of(own_parents)
    tree_scores = jnp.where(ancestry[:, None, :, :], tree_scores * score_scale, masked_value)
    local_top = jnp.maximum(jnp.max(cache_scores, axis=3), jnp.max(tree_scores, axis=3))
    row_top = over_copies(local_top, SEQ)
    cache_weights = jnp.exp(cache_scores - row_top[..., None])
    weight_sum = jnp.sum(cache_weights, axis=3)
    partial_value = jnp.einsum(
        "rhit,rtc->rhic",
        cache_weights.astype(jnp.bfloat16),
        cache_latent,
        preferred_element_type=jnp.float32,
    )
    head_first = seq_index * local_heads
    tree_mine = lax.dynamic_slice_in_dim(tree_scores, head_first, local_heads, 1)
    top_mine = lax.dynamic_slice_in_dim(row_top, head_first, local_heads, 1)
    tree_weights = jnp.exp(tree_mine - top_mine[..., None])
    tree_out = jnp.einsum(
        "rhij,rjc->rhic",
        tree_weights.astype(jnp.bfloat16),
        draft_latent,
        preferred_element_type=jnp.float32,
    )
    latent_sum, weight_total = (
        lax.psum_scatter(partial_value, SEQ, scatter_dimension=1, tiled=True),
        lax.psum_scatter(weight_sum, SEQ, scatter_dimension=1, tiled=True),
    )
    summed = jnp.einsum(
        "rhic,hcn->rhin", latent_sum + tree_out, absorb_v, preferred_element_type=jnp.float32
    )
    weight_total = weight_total + jnp.sum(tree_weights, axis=3)
    head_out = (summed / weight_total[..., None]).astype(jnp.bfloat16)
    head_rows = jnp.transpose(head_out, (0, 2, 1, 3)).reshape(
        requests * draft_count, local_heads * head_out.shape[3]
    )
    branch_term = jnp.dot(head_rows, out_proj, preferred_element_type=jnp.float32)
    width_local = residual.shape[1]
    feature_first = seq_index * width_local
    residual_wide = lax.dynamic_update_slice_in_dim(
        jnp.zeros_like(branch_term), residual.astype(jnp.float32), feature_first, 1
    )
    stream = lax.psum(branch_term + residual_wide, SEQ)
    square = jnp.sum(stream * stream, axis=1)
    normed = (
        stream * lax.rsqrt(square / stream.shape[1] + norm_epsilon)[:, None] * norm_gain
    ).astype(jnp.bfloat16)
    hidden_out = lax.dynamic_slice_in_dim(stream, feature_first, width_local, 1).astype(
        jnp.bfloat16
    )
    vocab_rows = lm_head.shape[0]
    vocab_first = lax.axis_index(SEQ_BATCH) * vocab_rows
    logits = jnp.einsum(
        "rd,vd->rv",
        lax.all_gather(normed, BATCH, axis=0, tiled=True),
        lm_head,
        preferred_element_type=jnp.float32,
    )
    request_total = parent.shape[0]
    parent_rows = (
        jnp.arange(request_total, dtype=jnp.int32)[:, None] * draft_count + parent
    ).reshape(-1)
    source = logits[parent_rows]
    column = jnp.arange(vocab_rows, dtype=jnp.int32) + vocab_first
    picked = jnp.sum(
        jnp.where(column[None, :] == draft_ids.reshape(-1)[:, None], source, 0.0), axis=1
    )
    local_best = jnp.max(logits, axis=1)
    local_mass = jnp.sum(jnp.exp(logits - local_best[:, None]), axis=1)
    best, exp_mass, chosen = combined_by_axis(
        (local_best, local_mass, picked), SEQ_BATCH, combine_soft
    )
    log_total = best + jnp.log(exp_mass)
    target_all = (chosen - log_total[parent_rows]).reshape(request_total, draft_count)
    target_logp = lax.dynamic_slice_in_dim(target_all, batch_index * requests, requests, 0)
    accepted_score = jnp.sum(
        jnp.where(
            jnp.arange(draft_count, dtype=jnp.int32)[None, :] < accept_len[:, None],
            target_logp,
            0.0,
        ),
        axis=1,
    )
    return (hidden_out, target_logp, accepted_score)


def solution(mesh):
    split = Mesh(mesh.devices.reshape(4, 4, 4, 2), ("seq_0", "seq_1", "batch_0", "batch_1"))
    in_specs = (
        P(BATCH, None, SEQ, None),
        P(BATCH, None, SEQ, None),
        P(SEQ, None, None),
        P(SEQ, None, None),
        P(BATCH, SEQ, None),
        P(BATCH, SEQ, None),
        P(BATCH, None, None),
        P(BATCH, None, None),
        P(BATCH, SEQ),
        P(SEQ, None),
        P(),
        P(SEQ_BATCH, None),
        P(),
        P(),
        P(BATCH),
        P(BATCH),
    )
    out_specs = (P(BATCH, SEQ), P(BATCH, None), P(BATCH))
    return jax.shard_map(body, mesh=split, in_specs=in_specs, out_specs=out_specs, check_vma=False)
```

profile of v0, /device:TPU:1, one launch (start us, length us, event | category | flops | bytes accessed | tf_op | source)
XLA Modules:
  0.0 529.6 jit_solution(17929896783594325636)
XLA Ops:
  7.2 1.0 copy.41
  8.2 1.6 fusion.16
  9.9 0.9 maximum_bitcast_fusion
  11.5 0.7 fusion.88
  12.2 0.2 fusion.39
  12.5 0.2 convolution_add_fusion.5
  12.7 0.2 fusion.99
  12.8 0.2 convolution_add_fusion.4
  13.2 0.2 convolution_add_fusion.3
  13.9 0.2 convolution_add_fusion.1
  14.0 0.2 fusion.17
  14.3 80.4 %all-gather.11.cloned.1.call-done = bf16[1,64,128,576]{3,1,0,2:T(8,128)(2,1)} async-done(((bf16[1,64,8,576]{3,1,0,2:T(8,128)(2,1)}), bf16[1,64,128,576]{3,1,0,2:T(8,128)(2,1)}) %all-gather.11.cloned.1.call-update) | async-done | bytes 9437200 | tf_op jit(solution)/shard_map/all_gather | solution.py:25
  94.7 1.8 split.9
  96.5 2.9 copy.69
  99.4 7.5 %fusion.10 = f32[64,128,64]{0,2,1:T(8,128)S(1)} fusion(bf16[1,64,512]{2,1,0:T(8,128)(2,1)S(1)} %copy-done.5, bf16[1,64,128,576]{3,1,0,2:T(8,128)(2,1)} %all-gather.11.cloned.1.call-done), kind=kOutput, calls=%fused_computation.11 | convolution fusion | flops 536870912 | bytes 10551296 | tf_op jit(solution)/shard_map/rihc,rjc->rhij/dot_general | solution.py:119
  106.9 5.8 %fusion.97 = (f32[128,64]{1,0:T(8,128)S(1)}, f32[1,128,64,64]{2,3,1,0:T(8,128)}) fusion(f32[64,128,64]{0,2,1:T(8,128)S(1)} %fusion.10, bf16[1,64,64]{2,1,0:T(8,128)(2,1)S(1)} %copy-done.8, bf16[1,64,128,576]{3,1,0,2:T(8,128)(2,1)} %all-gather.11.cloned.1.call-done, pred[64,64]{0,1:T(8,128)(4,1)S(1)} %copy.45), kind=kOutput, calls=%fused_computation.169 | convolution fusion | flops 69197824 | bytes 6336512 | tf_op jit(solution)/shard_map/rihe,rje->rhij/dot_general | solution.py:122
  112.8 7.7 %split.8 = bf16[1,64,128,512]{3,1,0,2:T(8,128)(2,1)} slice(bf16[1,64,128,576]{3,1,0,2:T(8,128)(2,1)} %all-gather.11.cloned.1.call-done), slice={[0:1], [0:64], [0:128], [0:512]} | slice | bytes 16777216 | tf_op jit(solution)/shard_map/split | solution.py:25
  120.5 30.0 %fusion.12 = f32[64,128,1024]{2,1,0:T(8,128)} fusion(bf16[1,64,128,512]{3,1,0,2:T(8,128)(2,1)} %split.8, bf16[1,1024,512]{2,1,0:T(8,128)(2,1)S(1)} %copy-done), kind=kOutput, calls=%fused_computation.14 | convolution fusion | flops 8589934592 | bytes 42991616 | tf_op jit(solution)/shard_map/rihc,rtc->rhit/dot_general | solution.py:110
  150.5 21.9 %fusion.96 = (f32[128,64]{0,1:T(8,128)S(1)}, f32[1,128,64,1024]{3,1,2,0:T(8,128)}) fusion(f32[64,128,1024]{2,1,0:T(8,128)} %fusion.12, bf16[1,1024,64]{1,2,0:T(8,128)(2,1)S(1)} %copy-done.4, bf16[1,64,128,64]{2,3,1,0:T(8,128)(2,1)S(1)} %copy-done.3, pred[1024]{0:T(1024)(128)(4,1)S(1)} %add_compare_fusion), kind=kOutput, calls=%fused_computation.168 | convolution fusion | flops 1107288064 | bytes 68322304 | tf_op jit(solution)/shard_map/rihe,rte->rhit/dot_general | solution.py:113
  172.5 15.1 %all_to_all.5 = f32[16,1,128,64]{2,3,1,0:T(8,128)S(1)} all-to-all(f32[16,1,128,64]{2,3,1,0:T(8,128)S(1)} %broadcast_in_dim.37), channel_id=1, replica_groups=mesh['seq_0'=4,'seq_1'=4,'batch_0'=4,'batch_1'=2] {'seq_0','seq_1'}, dimensions={0} | all-to-all | bytes 1048576 | tf_op jit(solution)/shard_map/all_to_all | solution.py:30
  187.7 18.7 %fusion.7 = f32[1,128,64,512]{3,1,2,0:T(8,128)} fusion(f32[1,128,64,1024]{3,1,2,0:T(8,128)} %get-tuple-element.19, f32[128,64]{0,1:T(8,128)S(1)} %reduce_max.38, bf16[1,1024,512]{2,1,0:T(8,128)(2,1)S(1)} %copy-done), kind=kOutput, calls=%fused_computation.10 | convolution fusion | flops 8606711808 | bytes 51412992 | tf_op jit(solution)/shard_map/rhit,rtc->rhic/dot_general | solution.py:132
  206.5 0.6 copy-done.12
  207.0 0.6 dynamic-slice.5
  208.4 1.0 fusion.24
  209.5 14.9 %fusion.1 = f32[128,64]{0,1:T(8,128)S(1)} fusion(f32[1,128,64,1024]{3,1,2,0:T(8,128)} %get-tuple-element.19, f32[128,64]{0,1:T(8,128)S(1)} %reduce_max.38), kind=kLoop, calls=%fused_computation.5 | loop fusion | flops 16769024 | bytes 33619968 | tf_op jit(solution)/shard_map/reduce_sum | solution.py:131
  224.6 58.5 %all-reduce = f32[1,128,64]{2,1,0:T(8,128)S(1)} all-reduce(f32[1,128,64]{2,1,0:T(8,128)S(1)} %copy.53), channel_id=7, replica_groups=mesh['seq_0'=4,'seq_1'=4,'batch_0'=4,'batch_1'=2] {'seq_0','seq_1'}, use_global_device_ids=true, to_apply=%region_5.6.clone | all-reduce | flops 8192 | bytes 65536
  283.4 33.9 %reduce-scatter.3.cloned.1.call-done = f32[1,8,64,512]{3,1,2,0:T(8,128)} async-done(((f32[1,128,64,512]{3,1,2,0:T(8,128)}), f32[1,8,64,512]{3,1,2,0:T(8,128)}) %reduce-scatter.3.cloned.1.call-update) | async-done | bytes 1048592 | tf_op jit(solution)/shard_map/reduce_scatter | solution.py:149
  317.3 1.5 fusion.15
  318.9 0.4 fusion.19
  319.4 7.9 %fusion.27 = f32[64,7168]{1,0:T(8,128)S(1)} fusion(bf16[1024,7168]{1,0:T(8,128)(2,1)} %param.25, bf16[8,8,8,128]{3,2,1,0:T(8,128)(2,1)S(1)} %bitcast.377), kind=kOutput, calls=%fused_computation.45 | convolution fusion | flops 939524096 | bytes 16646144 | tf_op jit(solution)/shard_map/dot_general | solution.py:160
  327.4 1.1 add.352
  328.5 1.2 copy-done.2
  329.8 88.2 %all-reduce.3.cloned.1.call-done = f32[64,7168]{1,0:T(8,128)} async-done(((f32[64,7168]{1,0:T(8,128)}), f32[64,7168]{1,0:T(8,128)}) %all-reduce.3.cloned.1.call-update) | async-done | bytes 1835024 | tf_op jit(solution)/shard_map/psum | solution.py:166
  418.0 1.7 multiply_reduce_fusion
  419.7 2.7 multiply_convert_fusion
  423.3 1.6 dynamic-slice_convert_fusion
  425.0 43.8 %all-gather.13.cloned.1.call-done = bf16[512,7168]{1,0:T(8,128)(2,1)} async-done(((bf16[64,7168]{1,0:T(8,128)(2,1)}), bf16[512,7168]{1,0:T(8,128)(2,1)}) %all-gather.13.cloned.1.call-update) | async-done | bytes 7340048 | tf_op jit(solution)/shard_map/all_gather | solution.py:178
  468.8 8.5 %fusion.98 = (f32[512]{0:T(512)S(1)}, f32[512,512]{0,1:T(8,128)S(1)}) fusion(bf16[512,7168]{1,0:T(8,128)(2,1)} %all-gather.13.cloned.1.call-done, bf16[512,7168]{1,0:T(8,128)(2,1)} %param.27), kind=kOutput, calls=%fused_computation.170 | convolution fusion | flops 3758358016 | bytes 15730688 | tf_op jit(solution)/shard_map/rd,vd->rv/dot_general | solution.py:176
  477.3 0.3 copy.58
  477.6 0.2 exponential_reduce_fusion
  477.8 1.6 gather_fusion
  479.5 0.3 select_reduce_fusion
  479.7 9.6 %all-gather.4 = f32[4,3,512]{2,1,0:T(4,128)S(1)} all-gather(f32[1,3,512]{2,1,0:T(4,128)S(1)} %maximum_bitcast_fusion.1), channel_id=2, replica_groups=mesh['seq_0'=4,'seq_1'=4,'batch_0'=4,'batch_1'=2] {'seq_0'}, dimensions={0}, use_global_device_ids=true | all-gather | bytes 30720 | tf_op jit(solution)/shard_map/all_gather | solution.py:46
  489.4 9.5 %all-gather.5 = f32[4,3,512]{2,1,0:T(4,128)S(1)} all-gather(f32[1,3,512]{2,1,0:T(4,128)S(1)} %maximum_bitcast_fusion.2), channel_id=3, replica_groups=mesh['seq_0'=4,'seq_1'=4,'batch_0'=4,'batch_1'=2] {'seq_1'}, dimensions={0}, use_global_device_ids=true | all-gather | bytes 30720 | tf_op jit(solution)/shard_map/all_gather | solution.py:46
  498.9 9.0 %all-gather.6 = f32[4,3,512]{2,1,0:T(4,128)S(1)} all-gather(f32[1,3,512]{2,1,0:T(4,128)S(1)} %maximum_bitcast_fusion.3), channel_id=4, replica_groups=mesh['seq_0'=4,'seq_1'=4,'batch_0'=4,'batch_1'=2] {'batch_0'}, dimensions={0}, use_global_device_ids=true | all-gather | bytes 30720 | tf_op jit(solution)/shard_map/all_gather | solution.py:46
  508.0 10.2 %all-gather.7 = f32[2,3,512]{2,1,0:T(4,128)S(1)} all-gather(f32[1,3,512]{2,1,0:T(4,128)S(1)} %maximum_bitcast_fusion.4), channel_id=5, replica_groups=mesh['seq_0'=4,'seq_1'=4,'batch_0'=4,'batch_1'=2] {'batch_1'}, dimensions={0}, use_global_device_ids=true | all-gather | bytes 18432 | tf_op jit(solution)/shard_map/all_gather | solution.py:46
  518.3 3.5 gather_fusion.1
  521.9 1.1 fusion.89
  (77 shorter events, 2.6 us)
Async XLA Ops:
  7.2 113.3 %copy-start = (bf16[1,1024,512]{2,1,0:T(8,128)(2,1)S(1)}, bf16[1,1024,512]{2,1,0:T(8,128)(2,1)}, u32[]{:S(2)}) copy-start(bf16[1,1024,512]{2,1,0:T(8,128)(2,1)} %param.20) | copy-start | bytes 3145732
  7.2 92.3 %copy-start.5 = (bf16[1,64,512]{2,1,0:T(8,128)(2,1)S(1)}, bf16[1,64,512]{2,1,0:T(8,128)(2,1)}, u32[]{:S(2)}) copy-start(bf16[1,64,512]{2,1,0:T(8,128)(2,1)} %param.22) | copy-start | bytes 196612
  7.2 87.5 %all-gather.11.cloned.1.call-start = ((), (), s32[]{:S(2)}) async-start(), calls=%async_computation.2 | async-start | bytes 11141120 | tf_op jit(solution)/shard_map/all_gather | solution.py:25
  10.8 306.5 %reduce-scatter.3.cloned.1.call-start = ((), (), s32[]{:S(2)}) async-start(), calls=%async_computation.3 | async-start | bytes 17825792 | tf_op jit(solution)/shard_map/reduce_scatter | solution.py:149
  96.5 10.4 %copy-start.8 = (bf16[1,64,64]{2,1,0:T(8,128)(2,1)S(1)}, bf16[1,64,64]{2,1,0:T(8,128)(2,1)}, u32[]{:S(2)}) copy-start(bf16[1,64,64]{2,1,0:T(8,128)(2,1)} %param.23) | copy-start | bytes 24580
  120.5 30.0 %copy-start.3 = (bf16[1,64,128,64]{2,3,1,0:T(8,128)(2,1)S(1)}, bf16[1,64,128,64]{2,3,1,0:T(8,128)(2,1)}, u32[]{:S(2)}) copy-start(bf16[1,64,128,64]{2,3,1,0:T(8,128)(2,1)} %copy.69) | copy-start | bytes 3145732
  120.5 30.0 %copy-start.4 = (bf16[1,1024,64]{1,2,0:T(8,128)(2,1)S(1)}, bf16[1,1024,64]{1,2,0:T(8,128)(2,1)}, u32[]{:S(2)}) copy-start(bf16[1,1024,64]{1,2,0:T(8,128)(2,1)} %param.21) | copy-start | bytes 393220
  206.4 0.7 copy-start.12
  206.4 211.5 %all-reduce.3.cloned.1.call-start = ((), (), s32[]{:S(2)}) async-start(), calls=%async_computation.4 | async-start | bytes 3670016 | tf_op jit(solution)/shard_map/psum | solution.py:166
  209.5 109.3 %copy-start.11 = (bf16[8,512,128]{2,1,0:T(8,128)(2,1)S(1)}, bf16[8,512,128]{2,1,0:T(8,128)(2,1)}, u32[]{:S(2)}) copy-start(bf16[8,512,128]{2,1,0:T(8,128)(2,1)} %param.19) | copy-start | bytes 3145732
  319.3 7.9 %copy-start.6 = (bf16[64,448]{1,0:T(8,128)(2,1)S(1)}, bf16[64,448]{1,0:T(8,128)(2,1)}, u32[]{:S(2)}) copy-start(bf16[64,448]{1,0:T(8,128)(2,1)} %param.24) | copy-start | bytes 172036
  319.3 100.3 %copy-start.7 = (f32[7168]{0:T(1024)S(1)}, f32[7168]{0:T(1024)}, u32[]{:S(2)}) copy-start(f32[7168]{0:T(1024)} %param.26) | copy-start | bytes 86020
  319.4 103.7 %copy-start.9 = (s32[8,64]{1,0:T(8,128)S(1)}, s32[8,64]{1,0:T(8,128)}, u32[]{:S(2)}) copy-start(s32[8,64]{1,0:T(8,128)} %param.29) | copy-start | bytes 6148
  319.4 103.8 %copy-start.10 = (s32[8,64]{1,0:T(8,128)S(1)}, s32[8,64]{1,0:T(8,128)}, u32[]{:S(2)}) copy-start(s32[8,64]{1,0:T(8,128)} %param.28) | copy-start | bytes 6148
  328.5 1.3 copy-start.2
  329.7 139.0 %all-gather.13.cloned.1.call-start = ((), (), s32[]{:S(2)}) async-start(), calls=%async_computation.5 | async-start | bytes 8257536 | tf_op jit(solution)/shard_map/all_gather | solution.py:178
  468.8 54.3 %copy-start.1 = (bf16[1,1024,512]{2,1,0:T(8,128)(2,1)S(1)}, bf16[1,1024,512]{2,1,0:T(8,128)(2,1)}, u32[]{:S(2)}) copy-start(bf16[1,1024,512]{2,1,0:T(8,128)(2,1)} %param.20) | copy-start | bytes 3145732
Sparse Core Ops, SparseCore 0:
  10.9 83.7 all-gather.10
  206.5 110.7 reduce-scatter.2
  329.9 88.0 all-reduce.2
  422.5 46.2 all-gather.12
where the time goes:
time: 530 us
  waiting for transfers between devices  246 us (46%)
  blocking collectives  112 us (21%)
  matrix products  106 us (20%)
  local copies, waits for them, and re-layouts  26 us (5%)
  other arithmetic  23.3 us (4%)
  between operations  16.1 us (3%)
    psum x1, waiting for transfers between devices, body(): stream = lax.psum(branch_term + residual_wide, SEQ)  88.2 us
    all_gather x1, waiting for transfers between devices, sent_together(): lax.all_gather(both, axis, axis=dim, tiled=True)  80.4 us
    unnamed x1, blocking collectives  58.5 us
    all_gather x1, waiting for transfers between devices, body(): lax.all_gather(normed, BATCH, axis=0, tiled=True)  43.8 us
    all_gather x4, blocking collectives, gathered_once(): both, at, found = (lax.all_gather(jnp.concatenate(lines), axis), 0, {})  38.3 us
    reduce_scatter x1, waiting for transfers between devices, body(): lax.psum_scatter(partial_value, SEQ, scatter_dimension=1, tiled=True)  33.9 us
    dot_general x1, matrix products, body(): jnp.einsum('rihc,rtc->rhit', query_all, cache_latent, preferred_element_t...  30 us
    dot_general x1, matrix products, body(): jnp.einsum('rihe,rte->rhit', rope_all, cache_rope, preferred_element_type...  21.9 us
  transfers between devices with their start and end apart: 4, of which 4 were waited for; matrix products, arithmetic and copies ran while one was open for 4% of the time, Pallas kernels for 0%

commit v1 on v0

--- a/solution.py
+++ b/solution.py
@@ -1,3 +1,4 @@
+import functools
 import math
 
 import jax
@@ -5,6 +6,262 @@
 from jax import lax
 from jax.sharding import Mesh
 from jax.sharding import PartitionSpec as P
+
+from jax.experimental import pallas as pl
+from jax.experimental.pallas import tpu as pltpu
+
+
+MESH_ID = pl.DeviceIdType.MESH
+LOWEST = -1e28
+MASKED = -1e30
+TRANS_B = (((1,), (1,)), ((), ()))
+
+
+def attention_kernel(scale, len_ref, q_ref, kl_ref, kr_ref, draft_ref, parent_ref, av_ref, out_ref,
+                     qbuf, kbuf, krbuf, avbuf, acc, top, mass, part, part_in, stat, stat_in, lse,
+                     loc_sem, q_send, q_recv, k_send, k_recv, r_send, r_recv, v_send, v_recv, p_send, p_recv):
+    y, z, c = lax.axis_index("seq_0"), lax.axis_index("seq_1"), lax.axis_index("batch_1")
+    turn = lambda at, by: lax.rem(at + by, 4)
+    y_right, y_left, y_far = {"seq_0": turn(y, 1)}, {"seq_0": turn(y, 3)}, {"seq_0": turn(y, 2)}
+    z_right, z_left = {"seq_1": turn(z, 1)}, {"seq_1": turn(z, 3)}
+    sibling = {"batch_1": 1 - c}
+    barrier = pltpu.get_barrier_semaphore()
+    for peer in (y_right, y_left, y_far, z_right, z_left, sibling):
+        pl.semaphore_signal(barrier, inc=1, device_id=peer, device_id_type=MESH_ID)
+    local = [
+        pltpu.make_async_copy(kl_ref.at[pl.ds(512 * h, 512)], kbuf.at[h, :, pl.ds(0, 512)], loc_sem.at[h])
+        for h in range(2)
+    ]
+    for copy in local:
+        copy.start()
+    own_av = pltpu.make_async_copy(av_ref, avbuf.at[0], loc_sem.at[2])
+    own_av.start()
+    own_q = pltpu.make_async_copy(q_ref, qbuf.at[0], loc_sem.at[3])
+    own_q.start()
+    own_r = pltpu.make_async_copy(kr_ref, krbuf.at[pl.ds(0, 2)], loc_sem.at[4])
+    own_r.start()
+    pl.semaphore_wait(barrier, 6)
+
+    def remote(src, dst, send, recv, peer):
+        copy = pltpu.make_async_remote_copy(src_ref=src, dst_ref=dst, send_sem=send, recv_sem=recv,
+                                            device_id=peer, device_id_type=MESH_ID)
+        copy.start()
+        return copy
+
+    half = lambda h: pl.ds(256 * h, 256)
+    sends = []
+    q_in, k_in, r_in = {}, {}, {}
+    for slot, peer, order in ((1, y_right, (0, 1)), (2, y_left, (1, 0))):
+        for h in order:
+            n = slot * 2 + h
+            q_in[n] = remote(q_ref.at[half(h)], qbuf.at[slot, half(h)], q_send.at[n], q_recv.at[n], peer)
+    for slot, peer, order in ((1, z_right, (0, 1)), (2, z_left, (1, 0))):
+        for h in order:
+            n = slot * 2 + h
+            k_in[n] = remote(kl_ref.at[pl.ds(512 * h, 512)], kbuf.at[n, :, pl.ds(0, 512)], k_send.at[n], k_recv.at[n], peer)
+            r_in[n] = remote(kr_ref.at[h], krbuf.at[n], r_send.at[n], r_recv.at[n], peer)
+
+    acc[...] = jnp.zeros_like(acc)
+    top[...] = jnp.full(top.shape, LOWEST, jnp.float32)
+    mass[...] = jnp.zeros_like(mass)
+
+    row = lax.broadcasted_iota(jnp.int32, (128, 128), 0)
+    col = lax.broadcasted_iota(jnp.int32, (128, 128), 1)
+    hop = ((parent_ref[...] == col) & (row > 0) & (row < 64)).astype(jnp.float32)
+    known = (row == col).astype(jnp.float32)
+    for _ in range(6):
+        step = hop.astype(jnp.bfloat16)
+        known = known + jnp.dot(known.astype(jnp.bfloat16), step, preferred_element_type=jnp.float32)
+        hop = jnp.dot(step, step, preferred_element_type=jnp.float32)
+    tree_bias = jnp.where((known > 0.5) & (col < 64), 0.0, MASKED)[:64]
+
+    def update(slot, rows, count, keys, values, bias):
+        width = bias.shape[1]
+        at = (slot, pl.ds(rows, count))
+        scores = lax.dot_general(qbuf[at], keys, TRANS_B, preferred_element_type=jnp.float32)
+        scores = scores * scale + bias
+        before = top[at]
+        now = jnp.maximum(before, jnp.max(scores, axis=1, keepdims=True))
+        weights = jnp.exp2(scores - jnp.tile(now, (1, width // 128)))
+        fade = jnp.exp2(before - now)
+        total = mass[at] * fade
+        for k in range(width // 128):
+            total = total + weights[:, 128 * k : 128 * k + 128]
+        mass[at] = total
+        top[at] = now
+        acc[at] = acc[at] * jnp.tile(fade, (1, 4)) + jnp.dot(
+            weights.astype(jnp.bfloat16), values, preferred_element_type=jnp.float32
+        )
+
+    own_q.wait()
+    for h in range(8):
+        update(0, 64 * h, 64, draft_ref[...], draft_ref[:, :512], tree_bias)
+
+    ROWS = 256
+
+    def chunks(first, count, slots_first, slots):
+        def chunk(kc, _):
+            source = lax.rem(z + jnp.where(kc // 2 == 0, 0, jnp.where(kc // 2 == 1, 3, jnp.where(kc // 2 == 2, 1, 2))), 4)
+            start = (y * 4 + source) * 1024 + lax.rem(kc, 2) * 512
+            spot = start + lax.broadcasted_iota(jnp.int32, (1, 512), 1)
+            bias = jnp.where(spot < len_ref[0], 0.0, MASKED)
+
+            def block(n, _):
+                update(slots_first + n // (512 // ROWS), pl.multiple_of(lax.rem(n, 512 // ROWS) * ROWS, ROWS), ROWS,
+                       kbuf[kc], kbuf[kc, :, :512], bias)
+                return 0
+
+            return lax.fori_loop(0, slots * (512 // ROWS), block, 0)
+
+        lax.fori_loop(first, first + count, chunk, 0)
+
+    def rope_in(n):
+        packed = krbuf[n].astype(jnp.float32)
+        kbuf[n, pl.ds(0, 256), pl.ds(512, 128)] = packed.astype(jnp.bfloat16)
+        kbuf[n, pl.ds(256, 256), pl.ds(512, 128)] = pltpu.roll(packed, 64, 1).astype(jnp.bfloat16)
+
+    for copy in local:
+        copy.wait()
+    own_r.wait()
+    for n in range(2):
+        rope_in(n)
+    chunks(0, 2, 0, 1)
+
+    q_in[2].wait_recv()
+    q_in[6] = remote(qbuf.at[1, half(0)], qbuf.at[3, half(0)], q_send.at[6], q_recv.at[6], y_right)
+    q_in[5].wait_recv()
+    q_in[7] = remote(qbuf.at[2, half(1)], qbuf.at[3, half(1)], q_send.at[7], q_recv.at[7], y_left)
+    q_in[3].wait_recv()
+    q_in[4].wait_recv()
+    chunks(0, 2, 1, 2)
+
+    def key_wait(n):
+        k_in[n].wait_recv()
+        r_in[n].wait_recv()
+
+    def key_on(n, m, peer):
+        k_in[m] = remote(kbuf.at[n, :, pl.ds(0, 512)], kbuf.at[m, :, pl.ds(0, 512)], k_send.at[m], k_recv.at[m], peer)
+        r_in[m] = remote(krbuf.at[n], krbuf.at[m], r_send.at[m], r_recv.at[m], peer)
+
+    key_wait(2)
+    key_on(2, 6, z_right)
+    key_wait(5)
+    key_on(5, 7, z_left)
+    rope_in(2)
+    rope_in(5)
+    chunks(2, 1, 0, 3)
+    chunks(5, 1, 0, 3)
+    q_in[6].wait_recv()
+    q_in[7].wait_recv()
+    v_in = {}
+    mine = 4 * c
+    pair = lambda first, h: pl.ds(first + 2 * h, 2)
+    for slot, peer, order in ((1, y_right, (0, 1)), (2, y_left, (1, 0))):
+        for h in order:
+            n = slot * 2 + h
+            v_in[n] = remote(av_ref.at[pair(mine, h)], avbuf.at[slot, pair(mine, h)], v_send.at[n], v_recv.at[n], peer)
+    chunks(0, 3, 3, 1)
+    chunks(5, 1, 3, 1)
+    v_in[2].wait_recv()
+    v_in[6] = remote(avbuf.at[1, pair(mine, 0)], avbuf.at[3, pair(mine, 0)], v_send.at[6], v_recv.at[6], y_right)
+    v_in[5].wait_recv()
+    v_in[7] = remote(avbuf.at[2, pair(mine, 1)], avbuf.at[3, pair(mine, 1)], v_send.at[7], v_recv.at[7], y_left)
+    key_wait(3)
+    key_wait(4)
+    rope_in(3)
+    rope_in(4)
+    chunks(3, 2, 0, 4)
+    v_in[3].wait_recv()
+    v_in[4].wait_recv()
+    v_over = {}
+    for slot in (1, 2):
+        v_over[slot] = remote(avbuf.at[slot, pl.ds(mine, 4)], avbuf.at[slot, pl.ds(mine, 4)], v_send.at[7 + slot], v_recv.at[7 + slot], sibling)
+    v_in[6].wait_recv()
+    v_in[7].wait_recv()
+    v_over[3] = remote(avbuf.at[3, pl.ds(mine, 4)], avbuf.at[3, pl.ds(mine, 4)], v_send.at[10], v_recv.at[10], sibling)
+    key_wait(6)
+    key_wait(7)
+    rope_in(6)
+    rope_in(7)
+    chunks(6, 2, 0, 4)
+    own_av.wait()
+    for slot in (1, 2, 3):
+        v_over[slot].wait_recv()
+
+    def finish(slot):
+        def head(h, _):
+            at = (slot, pl.ds(pl.multiple_of(64 * h, 64), 64))
+            total = jnp.sum(mass[at], axis=1, keepdims=True)
+            some = total > 0.0
+            safe = jnp.where(some, total, 1.0)
+            value = jnp.dot(acc[at].astype(jnp.bfloat16), avbuf[slot, h], preferred_element_type=jnp.float32)
+            part[at] = (value * jnp.where(some, 1.0 / safe, 0.0)).astype(jnp.bfloat16)
+            lse[pl.ds(pl.multiple_of(64 * h, 64), 64)] = jnp.where(some, top[at] + jnp.log2(safe), LOWEST)
+            return 0
+
+        lax.fori_loop(0, 8, head, 0)
+        for k in range(4):
+            stat[slot, pl.ds(k, 1)] = jnp.transpose(lse[pl.ds(128 * k, 128)])[:1]
+
+    p_in = []
+    for slot, place, peer in ((3, 3, y_far), (1, 2, y_left), (2, 1, y_right)):
+        finish(slot)
+        p_in.append(remote(part.at[slot], part_in.at[place], p_send.at[place], p_recv.at[place], peer))
+        p_in.append(remote(stat.at[slot], stat_in.at[place], p_send.at[place + 4], p_recv.at[place + 4], peer))
+    finish(0)
+    for copy in p_in:
+        copy.wait_recv()
+    levels = [stat[0, :4]] + [stat_in[k, :4] for k in (1, 2, 3)]
+    best = jnp.maximum(jnp.maximum(levels[0], levels[1]), jnp.maximum(levels[2], levels[3]))
+    shares = [jnp.exp2(level - best) for level in levels]
+    whole = 1.0 / (shares[0] + shares[1] + shares[2] + shares[3])
+    for k in range(4):
+        rows = pl.ds(128 * k, 128)
+        mixed = jnp.zeros((128, 128), jnp.float32)
+        for j in range(4):
+            share = jnp.transpose(jnp.broadcast_to((shares[j] * whole)[k : k + 1], (128, 128)))
+            block = part[0, rows] if j == 0 else part_in[j, rows]
+            mixed = mixed + share * block.astype(jnp.float32)
+        mixed = mixed.astype(jnp.bfloat16)
+        out_ref[:, pl.ds(256 * k, 128)] = mixed[:64]
+        out_ref[:, pl.ds(256 * k + 128, 128)] = mixed[64:]
+    for table in (q_in, k_in, r_in, v_in, v_over):
+        for copy in table.values():
+            copy.wait_send()
+    for copy in p_in:
+        copy.wait_send()
+
+
+def attention(q, kl, kr, draft, parent_col, absorb_v, cache_len, scale):
+    bf, f32 = jnp.bfloat16, jnp.float32
+    vm, hbm = pl.BlockSpec(memory_space=pltpu.VMEM), pl.BlockSpec(memory_space=pl.ANY)
+    dma = pltpu.SemaphoreType.DMA
+    return pl.pallas_call(
+        functools.partial(attention_kernel, scale * math.log2(math.e)),
+        out_shape=jax.ShapeDtypeStruct((64, 1024), bf),
+        in_specs=[pl.BlockSpec(memory_space=pltpu.SMEM), hbm, hbm, hbm, vm, vm, hbm],
+        out_specs=vm,
+        scratch_shapes=[
+            pltpu.VMEM((4, 512, 640), bf),
+            pltpu.VMEM((8, 512, 640), bf),
+            pltpu.VMEM((8, 256, 128), bf),
+            pltpu.VMEM((4, 8, 512, 128), bf),
+            pltpu.VMEM((4, 512, 512), f32),
+            pltpu.VMEM((4, 512, 128), f32),
+            pltpu.VMEM((4, 512, 128), f32),
+            pltpu.VMEM((4, 512, 128), bf),
+            pltpu.VMEM((4, 512, 128), bf),
+            pltpu.VMEM((4, 8, 128), f32),
+            pltpu.VMEM((4, 8, 128), f32),
+            pltpu.VMEM((512, 128), f32),
+            dma((5,)), dma((8,)), dma((8,)), dma((8,)), dma((8,)), dma((8,)), dma((8,)),
+            dma((11,)), dma((11,)), dma((8,)), dma((8,)),
+        ],
+        compiler_params=pltpu.CompilerParams(collective_id=1, has_side_effects=True, vmem_limit_bytes=40 << 20),
+        cost_estimate=pl.CostEstimate(flops=20_000_000_000, bytes_accessed=20_000_000, transcendentals=8_500_000),
+        name="attention",
+    )(cache_len, q, kl, kr, draft, parent_col, absorb_v)
+
 
 SEQ = ("seq_0", "seq_1")
 BATCH = ("batch_0", "batch_1")
@@ -99,64 +356,18 @@
     accept_len,
 ):
     requests, draft_count, local_heads, nope_width = q_nope.shape
-    cache_rows = cache_latent.shape[1]
     score_scale = 1.0 / math.sqrt(nope_width + q_rope.shape[3])
     seq_index = lax.axis_index(SEQ)
     batch_index = lax.axis_index(BATCH)
-    query_latent = jnp.einsum(
-        "rihn,hnc->rihc", q_nope, absorb_k, preferred_element_type=jnp.float32
-    ).astype(jnp.bfloat16)
-    query_all, rope_all = sent_together((query_latent, q_rope), SEQ, 2, 3)
-    cache_scores = jnp.einsum(
-        "rihc,rtc->rhit", query_all, cache_latent, preferred_element_type=jnp.float32
-    )
-    cache_scores = cache_scores + jnp.einsum(
-        "rihe,rte->rhit", rope_all, cache_rope, preferred_element_type=jnp.float32
-    )
-    positions = seq_index * cache_rows + jnp.arange(cache_rows, dtype=jnp.int32)
-    in_cache = positions[None, :] < cache_len[:, None]
-    cache_scores = jnp.where(in_cache[:, None, None, :], cache_scores * score_scale, masked_value)
-    tree_scores = jnp.einsum(
-        "rihc,rjc->rhij", query_all, draft_latent, preferred_element_type=jnp.float32
-    )
-    tree_scores = tree_scores + jnp.einsum(
-        "rihe,rje->rhij", rope_all, draft_rope, preferred_element_type=jnp.float32
-    )
-    own_parents = lax.dynamic_slice_in_dim(parent, batch_index * requests, requests, 0)
-    ancestry = ancestry_of(own_parents)
-    tree_scores = jnp.where(ancestry[:, None, :, :], tree_scores * score_scale, masked_value)
-    local_top = jnp.maximum(jnp.max(cache_scores, axis=3), jnp.max(tree_scores, axis=3))
-    row_top = over_copies(local_top, SEQ)
-    cache_weights = jnp.exp(cache_scores - row_top[..., None])
-    weight_sum = jnp.sum(cache_weights, axis=3)
-    partial_value = jnp.einsum(
-        "rhit,rtc->rhic",
-        cache_weights.astype(jnp.bfloat16),
-        cache_latent,
-        preferred_element_type=jnp.float32,
-    )
-    head_first = seq_index * local_heads
-    tree_mine = lax.dynamic_slice_in_dim(tree_scores, head_first, local_heads, 1)
-    top_mine = lax.dynamic_slice_in_dim(row_top, head_first, local_heads, 1)
-    tree_weights = jnp.exp(tree_mine - top_mine[..., None])
-    tree_out = jnp.einsum(
-        "rhij,rjc->rhic",
-        tree_weights.astype(jnp.bfloat16),
-        draft_latent,
-        preferred_element_type=jnp.float32,
-    )
-    latent_sum, weight_total = (
-        lax.psum_scatter(partial_value, SEQ, scatter_dimension=1, tiled=True),
-        lax.psum_scatter(weight_sum, SEQ, scatter_dimension=1, tiled=True),
-    )
-    summed = jnp.einsum(
-        "rhic,hcn->rhin", latent_sum + tree_out, absorb_v, preferred_element_type=jnp.float32
-    )
-    weight_total = weight_total + jnp.sum(tree_weights, axis=3)
-    head_out = (summed / weight_total[..., None]).astype(jnp.bfloat16)
-    head_rows = jnp.transpose(head_out, (0, 2, 1, 3)).reshape(
-        requests * draft_count, local_heads * head_out.shape[3]
-    )
+    bf = jnp.bfloat16
+    latent = jnp.einsum("ihn,hnc->hic", q_nope[0], absorb_k, preferred_element_type=jnp.float32)
+    rope = jnp.pad(jnp.transpose(q_rope[0], (1, 0, 2)), ((0, 0), (0, 0), (0, 64)))
+    query = jnp.concatenate([latent.astype(bf), rope], axis=2).reshape(512, 640)
+    kr = cache_rope[0].reshape(2, 2, 256, 64).transpose(0, 2, 1, 3).reshape(2, 256, 128)
+    draft = jnp.pad(jnp.concatenate([draft_latent[0], draft_rope[0]], axis=1), ((0, 64), (0, 64)))
+    own_parent = lax.dynamic_slice_in_dim(parent, batch_index, 1, 0)[0]
+    parent_col = jnp.broadcast_to(jnp.pad(own_parent, (0, 64))[:, None], (128, 128))
+    head_rows = attention(query, cache_latent[0], kr, draft, parent_col, absorb_v, cache_len, score_scale)
     branch_term = jnp.dot(head_rows, out_proj, preferred_element_type=jnp.float32)
     width_local = residual.shape[1]
     feature_first = seq_index * width_local

time: 530 us -> 294 us (0.55)
  waiting for transfers between devices: 246 us -> 137 us
  matrix products: 106 us -> 12.3 us
  blocking collectives: 112 us -> 38.3 us
  Pallas kernels: 0 us -> 73 us
  other arithmetic: 23.3 us -> 5.12 us
  local copies, waits for them, and re-layouts: 26 us -> 12 us
    dot_general x19 -> x1, matrix products: 89.3 us -> 1.2 us  [body(): jnp.einsum('ihn,hnc->hic', q_nope[0], absorb_k, preferred_element_type=jn...]
    all_gather x1 -> x0, waiting for transfers between devices: 80.4 us -> none  [sent_together(): lax.all_gather(both, axis, axis=dim, tiled=True)]
    pallas_call x0 -> x1, Pallas kernels: none -> 73 us  [attention(): pl.pallas_call(functools.partial(attention_kernel, scale * math.log2(math...]
    unnamed x1 -> x0, blocking collectives: 58.5 us -> none
    reduce_scatter x1 -> x0, waiting for transfers between devices: 33.9 us -> none  [body(): lax.psum_scatter(partial_value, SEQ, scatter_dimension=1, tiled=True)]
    reduce_sum x2 -> x0, other arithmetic: 15.9 us -> none  [the longest x1 14.9 us: body(): weight_sum = jnp.sum(cache_weights, axis=3)]
    all_to_all x1 -> x0, blocking collectives: 15.1 us -> none  [copy_for_each(): return lax.all_to_all(copies, axis, split_axis=0, concat_axis=0, tiled=True)]
    split x2 -> x0, local copies, waits for them, and re-layouts: 9.48 us -> none  [sent_together(): jnp.split(lax.all_gather(both, axis, axis=dim, tiled=True), ends, axis=al...]
  transfers between devices with their start and end apart: 4 -> 2, of which waited for: 4 -> 2; matrix products, arithmetic and copies ran while one was open for 4% -> 0% of each run, Pallas kernels for 0% -> 0%
where the time goes in v1:
time: 294 us
  waiting for transfers between devices  137 us (47%)
  Pallas kernels  73 us (25%)
  blocking collectives  38.3 us (13%)
  between operations  15.8 us (5%)
  matrix products  12.3 us (4%)
  local copies, waits for them, and re-layouts  12 us (4%)
  other arithmetic  5.12 us (2%)
    psum x1, waiting for transfers between devices, body(): stream = lax.psum(branch_term + residual_wide, SEQ)  92.3 us
    pallas_call x1, Pallas kernels, attention(): pl.pallas_call(functools.partial(attention_kernel, scale * math.log2(math...  73 us
    all_gather x1, waiting for transfers between devices, body(): lax.all_gather(normed, BATCH, axis=0, tiled=True)  44.7 us
    all_gather x4, blocking collectives, gathered_once(): both, at, found = (lax.all_gather(jnp.concatenate(lines), axis), 0, {})  38.3 us
    dot_general x1, matrix products, body(): jnp.einsum('rd,vd->rv', lax.all_gather(normed, BATCH, axis=0, tiled=True)...  8.44 us
  transfers between devices with their start and end apart: 2, of which 2 were waited for; matrix products, arithmetic and copies ran while one was open for 0% of the time, Pallas kernels for 0%

profile of v1, /device:TPU:1, one launch (start us, length us, event | category | flops | bytes accessed | tf_op | source)
XLA Modules:
  0.0 293.8 jit_solution(14684713624192997072)
XLA Ops:
  7.2 0.0 copy-start
  7.2 0.0 all-reduce.5.cloned.1.call-start
  8.0 0.9 copy.40
  8.9 1.0 reshape_squeeze.3
  9.9 0.0 copy-start.8
  9.9 0.0 copy-start.1
  9.9 0.0 copy-start.2
  9.9 0.1 copy.35.kr_ref
  10.1 0.0 copy-start.6
  10.1 0.8 fusion.51
  10.9 1.2 convolution_convert_fusion
  12.1 0.0 slice-start
  12.1 0.1 fusion.1
  12.3 0.1 broadcast_in_dim.8.parent_ref
  12.4 0.0 slice-start.1
  12.4 0.0 slice-start.2
  12.4 73.0 %attention.1 = bf16[64,1024]{1,0:T(8,128)(2,1)S(1)} custom-call(s32[1]{0:T(128)S(6)} %copy.43.len_ref, bf16[512,640]{1,0:T(8,128)(2,1)S(1)} %bitcast.262, bf16[1024,512]{1,0:T(8,128)(2,1)S(1)} %bitcast.263, bf16[2,256,128]{2,1,0:T(8,128)(2,1)S(1)} %copy.35.kr_ref, bf16[128,640]{1,0:T(8,128)(2,1)S(1)} %fusion.7.draft_ref, ...), custom_call_target="tpu_custom_call" | custom-call | flops 20000000000 | bytes 20000000 | tf_op jit(solution)/shard_map/attention/pallas_call | solution.py:239
  85.4 0.0 copy-start.5
  85.4 2.7 fusion.58
  88.1 0.1 convert_add_fusion
  88.2 1.1 add.284
  89.3 0.0 copy-start.7
  89.3 1.2 copy-done.3
  90.5 0.0 all-reduce.5.cloned.1.call-update
  90.6 0.2 all-gather.10.cloned.1.call-start
  90.8 92.3 %all-reduce.5.cloned.1.call-done = f32[64,7168]{1,0:T(8,128)} async-done(((f32[64,7168]{1,0:T(8,128)}), f32[64,7168]{1,0:T(8,128)}) %all-reduce.5.cloned.1.call-update) | async-done | bytes 1835024 | tf_op jit(solution)/shard_map/psum | solution.py:377
  183.1 1.9 multiply_reduce_fusion
  185.0 0.2 copy-done.4
  185.2 1.2 multiply_convert_fusion
  186.4 0.0 all-gather.10.cloned.1.call-update
  187.1 0.1 broadcast_add_fusion
  187.1 0.1 reshape.820
  187.2 0.1 eq.16
  187.3 0.7 dynamic-slice_convert_fusion
  188.0 44.7 %all-gather.10.cloned.1.call-done = bf16[512,7168]{1,0:T(8,128)(2,1)} async-done(((bf16[64,7168]{1,0:T(8,128)(2,1)}), bf16[512,7168]{1,0:T(8,128)(2,1)}) %all-gather.10.cloned.1.call-update) | async-done | bytes 7340048 | tf_op jit(solution)/shard_map/all_gather | solution.py:389
  232.8 8.4 %fusion.57 = (f32[512]{0:T(512)S(1)}, f32[512,512]{0,1:T(8,128)S(1)}) fusion(bf16[512,7168]{1,0:T(8,128)(2,1)} %all-gather.10.cloned.1.call-done, bf16[512,7168]{1,0:T(8,128)(2,1)} %param.27), kind=kOutput, calls=%fused_computation.116 | convolution fusion | flops 3758358016 | bytes 15730688 | tf_op jit(solution)/shard_map/rd,vd->rv/dot_general | solution.py:387
  241.2 0.3 copy.36
  241.6 0.2 exponential_reduce_fusion
  241.8 1.6 gather_fusion
  243.4 0.3 select_reduce_fusion
  243.7 9.6 %all-gather.4 = f32[4,3,512]{2,1,0:T(4,128)S(1)} all-gather(f32[1,3,512]{2,1,0:T(4,128)S(1)} %maximum_bitcast_fusion), channel_id=2, replica_groups=mesh['seq_0'=4,'seq_1'=4,'batch_0'=4,'batch_1'=2] {'seq_0'}, dimensions={0}, use_global_device_ids=true | all-gather | bytes 30720 | tf_op jit(solution)/shard_map/all_gather | solution.py:303
  253.4 9.5 %all-gather.5 = f32[4,3,512]{2,1,0:T(4,128)S(1)} all-gather(f32[1,3,512]{2,1,0:T(4,128)S(1)} %maximum_bitcast_fusion.1), channel_id=3, replica_groups=mesh['seq_0'=4,'seq_1'=4,'batch_0'=4,'batch_1'=2] {'seq_1'}, dimensions={0}, use_global_device_ids=true | all-gather | bytes 30720 | tf_op jit(solution)/shard_map/all_gather | solution.py:303
  262.9 9.0 %all-gather.6 = f32[4,3,512]{2,1,0:T(4,128)S(1)} all-gather(f32[1,3,512]{2,1,0:T(4,128)S(1)} %maximum_bitcast_fusion.2), channel_id=4, replica_groups=mesh['seq_0'=4,'seq_1'=4,'batch_0'=4,'batch_1'=2] {'batch_0'}, dimensions={0}, use_global_device_ids=true | all-gather | bytes 30720 | tf_op jit(solution)/shard_map/all_gather | solution.py:303
  272.0 10.2 %all-gather.7 = f32[2,3,512]{2,1,0:T(4,128)S(1)} all-gather(f32[1,3,512]{2,1,0:T(4,128)S(1)} %maximum_bitcast_fusion.3), channel_id=5, replica_groups=mesh['seq_0'=4,'seq_1'=4,'batch_0'=4,'batch_1'=2] {'batch_1'}, dimensions={0}, use_global_device_ids=true | all-gather | bytes 18432 | tf_op jit(solution)/shard_map/all_gather | solution.py:303
  282.2 0.1 add.316
  282.3 3.5 %gather_fusion.1 = f32[512]{0:T(512)S(1)} fusion(f32[512]{0:T(512)S(1)} %log_add_fusion, s32[1024]{0:T(1024)S(1)} %pad_clamp_fusion), kind=kCustom, calls=%fused_computation.1 | custom fusion | bytes 6144 | tf_op jit(solution)/shard_map/gather | solution.py:408
  285.8 0.1 gather.10
  285.9 1.1 fusion.52
  (40 shorter events, 0.3 us)
Async XLA Ops:
  7.2 3.8 %copy-start = (bf16[8,128,512]{2,1,0:T(8,128)(2,1)S(1)}, bf16[8,128,512]{2,1,0:T(8,128)(2,1)}, u32[]{:S(2)}) copy-start(bf16[8,128,512]{2,1,0:T(8,128)(2,1)} %param.18) | copy-start | bytes 3145732
  7.2 176.0 %all-reduce.5.cloned.1.call-start = ((), (), s32[]{:S(2)}) async-start(), calls=%async_computation | async-start | bytes 3670016 | tf_op jit(solution)/shard_map/psum | solution.py:377
  9.9 2.3 copy-start.8
  9.9 2.4 copy-start.1
  9.9 2.4 copy-start.2
  10.1 2.2 copy-start.6
  12.1 73.2 %slice-start = ((s8[14680064]{0:T(1024)(128)(4,1)}), s8[4194304]{0:T(1024)(128)(4,1)S(1)}, s32[]{:S(2)}) async-start(s8[14680064]{0:T(1024)(128)(4,1)} %bitcast.264), calls=%async_computation.2 | async-start | bytes 8388608
  12.4 73.0 %slice-start.1 = ((s8[14680064]{0:T(1024)(128)(4,1)}), s8[4194304]{0:T(1024)(128)(4,1)S(1)}, s32[]{:S(2)}) async-start(s8[14680064]{0:T(1024)(128)(4,1)} %bitcast.264), calls=%async_computation.3 | async-start | bytes 8388608
  12.4 73.0 %slice-start.2 = ((s8[14680064]{0:T(1024)(128)(4,1)}), s8[4194304]{0:T(1024)(128)(4,1)S(1)}, s32[]{:S(2)}) async-start(s8[14680064]{0:T(1024)(128)(4,1)} %bitcast.264), calls=%async_computation.4 | async-start | bytes 8388608
  12.4 73.0 %slice-start.3 = ((s8[14680064]{0:T(1024)(128)(4,1)}), s8[2097152]{0:T(1024)(128)(4,1)S(1)}, s32[]{:S(2)}) async-start(s8[14680064]{0:T(1024)(128)(4,1)} %bitcast.264), calls=%async_computation.5 | async-start | bytes 4194304
  85.4 2.7 copy-start.5
  89.3 1.2 copy-start.3
  89.3 95.7 %copy-start.7 = (f32[7168]{0:T(1024)S(1)}, f32[7168]{0:T(1024)}, u32[]{:S(2)}) copy-start(f32[7168]{0:T(1024)} %param.26) | copy-start | bytes 86020
  90.6 142.2 %all-gather.10.cloned.1.call-start = ((), (), s32[]{:S(2)}) async-start(), calls=%async_computation.1 | async-start | bytes 8257536 | tf_op jit(solution)/shard_map/all_gather | solution.py:389
  183.1 2.1 copy-start.4
  185.2 1.9 copy-start.10
  185.2 2.0 copy-start.9
Sparse Core Ops, SparseCore 0:
  90.7 92.3 all-reduce.4
  186.5 46.2 all-gather.9

commit v2 on v1

--- a/solution.py
+++ b/solution.py
@@ -4,12 +4,16 @@
 import jax
 import jax.numpy as jnp
 from jax import lax
+from jax.experimental import pallas as pl
+from jax.experimental.pallas import tpu as pltpu
 from jax.sharding import Mesh
 from jax.sharding import PartitionSpec as P
 
-from jax.experimental import pallas as pl
-from jax.experimental.pallas import tpu as pltpu
-
+SEQ = ("seq_0", "seq_1")
+BATCH = ("batch_0", "batch_1")
+SEQ_BATCH = ("seq_0", "seq_1", "batch_0", "batch_1")
+
+norm_epsilon = 1e-06
 
 MESH_ID = pl.DeviceIdType.MESH
 LOWEST = -1e28
@@ -263,78 +267,320 @@
     )(cache_len, q, kl, kr, draft, parent_col, absorb_v)
 
 
-SEQ = ("seq_0", "seq_1")
-BATCH = ("batch_0", "batch_1")
-SEQ_BATCH = ("seq_0", "seq_1", "batch_0", "batch_1")
-
-
-masked_value = -1e30
-norm_epsilon = 1e-06
-highest = lax.Precision.HIGHEST
-
-
-def sent_together(arrays, axis, dim, along):
-    ends, at = ([], 0)
-    for a in arrays[:-1]:
-        at += a.shape[along]
-        ends.append(at)
-    both = jnp.concatenate(arrays, axis=along)
-    return tuple(jnp.split(lax.all_gather(both, axis, axis=dim, tiled=True), ends, axis=along))
-
-
-def copy_for_each(array, axis):
-    copies = jnp.broadcast_to(array, (lax.axis_size(axis), *array.shape))
-    return lax.all_to_all(copies, axis, split_axis=0, concat_axis=0, tiled=True)
-
-
-def over_copies(array, axis):
-    everything = copy_for_each(array, axis)
-    return jnp.max(everything, axis=0)
-
-
-def gathered_once(array, axis):
-    leaves = jax.tree.leaves(array)
-    sequence = sorted(range(len(leaves)), key=lambda k: -leaves[k].size)
-    width = (1, *leaves[sequence[0]].shape)[-1]
-    lines = [
-        jnp.pad(leaves[k].reshape(-1), (0, -leaves[k].size % width)).reshape(-1, width)
-        for k in sequence
-    ]
-    both, at, found = (lax.all_gather(jnp.concatenate(lines), axis), 0, {})
-    for k, line in zip(sequence, lines):
-        piece = both[:, at : at + len(line)].reshape(len(both), -1)
-        found[k] = piece[:, : leaves[k].size].reshape(-1, *leaves[k].shape)
-        at += len(line)
-    numbers = iter(range(len(leaves)))
-    return jax.tree.map(lambda _: found[next(numbers)], array)
-
-
-def combined_by_axis(array, axes, combine):
-    for axis in axes:
-        pieces = gathered_once(array, axis)
-        array = jax.tree.map(lambda part: part[0], pieces)
-        for k in range(1, lax.axis_size(axis)):
-            array = combine(array, jax.tree.map(lambda part: part[k], pieces))
-    return array
-
-
-def ancestry_of(parents):
-    draft_count = parents.shape[1]
-    indices = jnp.arange(draft_count, dtype=jnp.int32)
-    parent_map = (
-        (parents[:, :, None] == indices[None, None, :]) & (indices[None, :, None] > 0)
-    ).astype(jnp.float32)
-    ancestry = jnp.broadcast_to(jnp.eye(draft_count, dtype=jnp.float32), parent_map.shape)
-    for doubling in range(draft_count.bit_length() - 1):
-        ancestry = ancestry + jnp.einsum("rij,rjk->rik", ancestry, parent_map, precision=highest)
-        parent_map = jnp.einsum("rij,rjk->rik", parent_map, parent_map, precision=highest)
-    return ancestry > 0.5
-
-
-def combine_soft(earlier, later):
-    top_new = jnp.maximum(earlier[0], later[0])
-    mass_new = earlier[1] * jnp.exp(earlier[0] - top_new) + later[1] * jnp.exp(later[0] - top_new)
-    return (top_new, mass_new, earlier[2] + later[2])
+def head_kernel(rows_ref, proj_ref, resid_ref, gain_ref, lm_ref, table_ref, accept_ref,
+                hid_ref, target_ref, score_ref,
+                part, part_in, near, near_in, hid_own, wide, lm, logits, tile, tile1, tile2,
+                lm_sem, s_send, s_recv, n_sem, h_sem, g1_send, g1_recv, g2_send, g2_recv, g3_send, g3_recv,
+                c_send, c_recv, f1_send, f1_recv, f2_send, f2_recv):
+    y, z = lax.axis_index("seq_0"), lax.axis_index("seq_1")
+    x, c = lax.axis_index("batch_0"), lax.axis_index("batch_1")
+    zh, zl = z // 2, lax.rem(z, 2)
+    me, group, place = y * 4 + z, y * 2 + z // 2, x * 2 + c
+    bf, f32 = jnp.bfloat16, jnp.float32
+    lm_copy = pltpu.make_async_copy(lm_ref, lm, lm_sem)
+    lm_copy.start()
+
+    def seq_peer(s):
+        return {"seq_0": s // 4, "seq_1": lax.rem(s, 4)}
+
+    def batch_peer(b):
+        return {"batch_0": b // 2, "batch_1": lax.rem(b, 2)}
+
+    barrier = pltpu.get_barrier_semaphore()
+
+    def greet_seq(k, _):
+        pl.semaphore_signal(barrier, inc=1, device_id=seq_peer(lax.rem(me + k, 16)), device_id_type=MESH_ID)
+        return 0
+
+    def greet_batch(k, _):
+        pl.semaphore_signal(barrier, inc=1, device_id=batch_peer(lax.rem(place + k, 8)), device_id_type=MESH_ID)
+        return 0
+
+    lax.fori_loop(1, 16, greet_seq, 0)
+    lax.fori_loop(1, 8, greet_batch, 0)
+
+    def describe(src, dst, send, recv, peer):
+        return pltpu.make_async_remote_copy(src_ref=src, dst_ref=dst, send_sem=send, recv_sem=recv,
+                                            device_id=peer, device_id_type=MESH_ID)
+
+    def remote(*spec):
+        copy = describe(*spec)
+        copy.start()
+        return copy
+
+    def product(g):
+        return jnp.dot(rows_ref[...], proj_ref[:, pl.ds(pl.multiple_of(g * 896, 128), 896)], preferred_element_type=f32)
+
+    def outward(s):
+        return describe(part.at[s], part_in.at[me], s_send.at[s], s_recv.at[me], seq_peer(s))
+
+    def inward(s):
+        return describe(part.at[s], part_in.at[s], s_send.at[s], s_recv.at[s], seq_peer(s))
+
+    def make(g):
+        block = product(g).astype(bf)
+        part[2 * g] = block[:32]
+        part[2 * g + 1] = block[32:]
+
+    make(lax.rem(group + 1, 8))
+    pl.semaphore_wait(barrier, 22)
+
+    def spread(k, _):
+        g = lax.rem(group + k, 8)
+        outward(2 * g).start()
+        outward(2 * g + 1).start()
+
+        @pl.when(k < 7)
+        def _():
+            make(lax.rem(group + k + 1, 8))
+
+        return 0
+
+    lax.fori_loop(1, 8, spread, 0)
+    mine = product(group) + resid_ref[...].astype(f32)
+    first = zl == 0
+    near[...] = jnp.where(first, mine[32:], mine[:32])
+    partner = {"seq_1": zh * 2 + 1 - zl}
+    near_copy = remote(near, near_in, n_sem.at[0], n_sem.at[1], partner)
+    stream = jnp.where(first, mine[:32], mine[32:])
+    other = group * 2
+
+    def collect(k, total):
+        s = lax.rem(other + 1 + k, 16)
+        inward(s).wait_recv()
+        return total + part_in[s].astype(f32)
+
+    stream = lax.fori_loop(1, 15, collect, stream)
+    near_copy.wait_recv()
+    stream = stream + near_in[...]
+
+    squares = jnp.sum(stream * stream, axis=1, keepdims=True)
+    high = squares.astype(bf)
+    low = (squares - high.astype(f32)).astype(bf)
+    lane = lax.broadcasted_iota(jnp.int32, (32, 128), 1)
+    at = (y, zh, x, c, zl)
+    wide[(*at, slice(None), pl.ds(0, 896))] = (stream * gain_ref[:, pl.ds(pl.multiple_of(group * 896, 128), 896)]).astype(bf)
+    wide[(*at, slice(None), pl.ds(896, 128))] = jnp.where(lane < 64, high.astype(f32), low.astype(f32)).astype(bf)
+
+    lanes = (pl.ds(0, 384), pl.ds(384, 384), pl.ds(768, 256))
+    every = slice(None)
+    along = {"x": ("batch_0", x), "y": ("seq_0", y), "z": ("seq_1", z)}
+
+    def turned(axis, by):
+        name, own = along[axis]
+        return {name: lax.rem(own + by, 4)}
+
+    def view(p, done, pos, half=None):
+        py, pz, px = pos["y"], pos["z"], pos["x"]
+        iy = every if "y" in done else py
+        izh, izl = (every, every) if "z" in done else (pz // 2, lax.rem(pz, 2))
+        ix = every if "x" in done else px
+        if half is not None:
+            if "y" in done:
+                iy = pl.ds(2 * half, 2)
+            else:
+                izh = pl.ds(half, 1)
+        return wide.at[iy, izh, ix, pos.get("c", c), izl, :, lanes[p]]
+
+    orders = (("x", "y", "z"), ("y", "z", "x"), ("z", "x", "y"))
+    here = {"x": x, "y": y, "z": z}
+
+    def moved(axis, by):
+        return {**here, axis: lax.rem(here[axis] + by, 4)}
+
+    pending = []
+    hid_own[...] = stream.astype(bf)
+    hid_copy = None
+    waits = {}
+    for stage, (sends, recvs) in enumerate(((g1_send, g1_recv), (g2_send, g2_recv))):
+        for p in range(3):
+            axis, done = orders[p][stage], orders[p][:stage]
+            for k in (1, 3, 2):
+                n = p * 3 + k - 1
+                own = view(p, done, here)
+                copy = remote(own, own, sends.at[n], recvs.at[n], turned(axis, k))
+                pending.append(copy)
+                waits[stage, p, k] = (done, axis, n, sends, recvs)
+        if stage == 0:
+            hid_copy = remote(hid_own, hid_ref.at[zl], h_sem.at[0], h_sem.at[1], partner)
+            hid_ref[zl] = hid_own[...]
+        for p in range(3):
+            done, axis = orders[p][:stage], orders[p][stage]
+            for k in (1, 3, 2):
+                n = p * 3 + k - 1
+                came = view(p, done, moved(axis, 4 - k))
+                describe(came, came, sends.at[n], recvs.at[n], turned(axis, k)).wait_recv()
+    sibling = {"batch_1": 1 - c}
+
+    def over(p, n, which):
+        copy = remote(which, which, c_send.at[n], c_recv.at[n], sibling)
+        pending.append(copy)
+
+    for p in range(3):
+        axis, done = orders[p][2], orders[p][:2]
+        for k, halves in ((1, (0, 1)), (3, (1, 0))):
+            for half in halves:
+                n = p * 6 + (k // 2) * 2 + half
+                own = view(p, done, here, half)
+                pending.append(remote(own, own, g3_send.at[n], g3_recv.at[n], turned(axis, k)))
+    for p in range(3):
+        over(p, p * 4, view(p, orders[p][:2], here))
+
+    def came3(p, k, half):
+        axis, done = orders[p][2], orders[p][:2]
+        n = p * 6 + {1: 0, 3: 2, 2: 4}[k] + half
+        block = view(p, done, moved(axis, 4 - k), half)
+        describe(block, block, g3_send.at[n], g3_recv.at[n], turned(axis, 1)).wait_recv()
+        return block
+
+    def column(r):
+        return jnp.transpose(jnp.broadcast_to(table_ref[pl.ds(r, 1)], (128, 128)))
+
+    for p in range(3):
+        axis = orders[p][2]
+        block = came3(p, 1, 0)
+        pending.append(remote(block, block, g3_send.at[p * 6 + 4], g3_recv.at[p * 6 + 4], turned(axis, 1)))
+        block = came3(p, 3, 1)
+        pending.append(remote(block, block, g3_send.at[p * 6 + 5], g3_recv.at[p * 6 + 5], turned(axis, 3)))
+    for p in range(3):
+        axis, done = orders[p][2], orders[p][:2]
+        came3(p, 1, 1)
+        over(p, p * 4 + 1, view(p, done, moved(axis, 3)))
+        came3(p, 3, 0)
+        over(p, p * 4 + 2, view(p, done, moved(axis, 1)))
+    for p in range(3):
+        axis, done = orders[p][2], orders[p][:2]
+        came3(p, 2, 0)
+        came3(p, 2, 1)
+        over(p, p * 4 + 3, view(p, done, moved(axis, 2)))
+    for p in range(3):
+        axis, done = orders[p][2], orders[p][:2]
+        for n, by in ((0, 0), (1, 3), (2, 1), (3, 2)):
+            block = view(p, done, {**moved(axis, by), "c": 1 - c})
+            describe(block, block, c_send.at[p * 4 + n], c_recv.at[p * 4 + n], sibling).wait_recv()
+    lm_copy.wait()
+
+    logits[...] = jnp.zeros_like(logits)
+    tile[...] = jnp.zeros_like(tile)
+
+    def contract(g, squares):
+        left = wide[g // 2, lax.rem(g, 2)].reshape(512, 1024)
+        right = lm[:, pl.ds(pl.multiple_of(g * 896, 128), 896)]
+        logits[...] += lax.dot_general(left[:, :896], right, TRANS_B, preferred_element_type=f32)
+        return squares + left[:, 896:].astype(f32)
+
+    squares = lax.fori_loop(0, 8, contract, jnp.zeros((512, 128), f32))
+    squares = jnp.sum(squares, axis=1, keepdims=True) * (1.0 / 64)
+    rate = lax.rsqrt(squares * (1.0 / 7168) + norm_epsilon)
+    vocab_first = (me * 8 + place) * 512
+    entry = lax.broadcasted_iota(jnp.int32, (64, 512), 1) + vocab_first
+    spot = lax.broadcasted_iota(jnp.int32, (64, 128), 1)
+    for k in range(4):
+        parents, wanted = column(k), column(4 + k)
+        bests, masses, picks = [], [], []
+        for h in range(2):
+            rows = slice(128 * k + 64 * h, 128 * k + 64 * h + 64)
+            values = logits[rows] * rate[rows]
+            best = jnp.max(values, axis=1, keepdims=True)
+            mass = jnp.sum(jnp.exp(values - best), axis=1, keepdims=True)
+            choose = (parents[64 * h : 64 * h + 64].astype(jnp.int32) == spot).astype(bf)[:, :64]
+            rest, source = values, jnp.zeros((64, 512), f32)
+            for _ in range(3):
+                piece = rest.astype(bf)
+                source = source + jnp.dot(choose, piece, preferred_element_type=f32)
+                rest = rest - piece.astype(f32)
+            hit = entry == jnp.tile(wanted[64 * h : 64 * h + 64].astype(jnp.int32), (1, 4))
+            pick = jnp.sum(jnp.where(hit, source, 0.0), axis=1, keepdims=True)
+            for found, one in ((bests, best), (masses, mass), (picks, pick)):
+                found.append(jnp.broadcast_to(one, (64, 128)))
+        for i, found in enumerate((bests, masses, picks)):
+            tile[pl.ds(4 * i + k, 1)] = jnp.transpose(jnp.concatenate(found, axis=0))[:1]
+
+    def merge(blocks):
+        best = functools.reduce(jnp.maximum, [b[0:4] for b in blocks])
+        mass = sum(b[4:8] * jnp.exp(b[0:4] - best) for b in blocks)
+        return best, mass, sum(b[8:12] for b in blocks)
+
+    def exchange(landing, sends, recvs, count, own, peer):
+        for k in range(1, count):
+            pending.append(remote(tile, landing.at[k], sends.at[k], recvs.at[k], peer(lax.rem(own + k, count))))
+        found = [tile[...]]
+        for k in range(1, count):
+            describe(tile, landing.at[k], sends.at[k], recvs.at[k], peer(lax.rem(own + k, count))).wait_recv()
+            found.append(landing[k])
+        for copy in pending[1 - count :]:
+            copy.wait_send()
+        del pending[1 - count :]
+        return merge(found)
+
+    best, mass, pick = exchange(tile1, f1_send, f1_recv, 8, place, batch_peer)
+    tile[pl.ds(0, 4)] = best
+    tile[pl.ds(4, 4)] = mass
+    tile[pl.ds(8, 4)] = pick
+    best, mass, pick = exchange(tile2, f2_send, f2_recv, 16, me, seq_peer)
+    total = best + jnp.log(mass)
+
+    def own_row(values):
+        line = lax.broadcasted_iota(jnp.int32, (4, 128), 0)
+        row = jnp.sum(jnp.where(line == x, values, 0.0), axis=0, keepdims=True)
+        row = jnp.broadcast_to(row, (128, 128))
+        return jnp.where(c == 0, row, pltpu.roll(row, 64, 1))
+
+    lane = lax.broadcasted_iota(jnp.int32, (128, 128), 1)
+    parents = jnp.transpose(own_row(table_ref[0:4])).astype(jnp.int32)
+    of_parent = jnp.sum(jnp.where((parents == lane) & (lane < 64), own_row(total), 0.0), axis=1, keepdims=True)
+    of_parent = jnp.transpose(jnp.broadcast_to(of_parent, (128, 128)))[:8]
+    target = own_row(pick)[:8] - of_parent
+    target_ref[...] = target
+    kept = lane[:8] < jnp.minimum(accept_ref[0], 64)
+    score_ref[...] = jnp.broadcast_to(jnp.sum(jnp.where(kept, target, 0.0), axis=1, keepdims=True), (8, 128))
+
+    hid_back = describe(hid_own, hid_ref.at[1 - zl], h_sem.at[0], h_sem.at[1], partner)
+    hid_back.wait_recv()
+    hid_copy.wait_send()
+    near_copy.wait_send()
+
+    def sent(k, _):
+        outward(lax.rem(other + 1 + k, 16)).wait_send()
+        return 0
+
+    lax.fori_loop(1, 15, sent, 0)
+    for copy in pending:
+        copy.wait_send()
+
+
+def head(rows, proj, resid, gain, lm_head, table, accept):
+    bf, f32 = jnp.bfloat16, jnp.float32
+    vm, hbm = pl.BlockSpec(memory_space=pltpu.VMEM), pl.BlockSpec(memory_space=pl.ANY)
+    dma = pltpu.SemaphoreType.DMA
+    return pl.pallas_call(
+        head_kernel,
+        out_shape=(
+            jax.ShapeDtypeStruct((2, 32, 896), bf),
+            jax.ShapeDtypeStruct((8, 128), f32),
+            jax.ShapeDtypeStruct((8, 128), f32),
+        ),
+        in_specs=[vm, vm, vm, vm, hbm, vm, pl.BlockSpec(memory_space=pltpu.SMEM)],
+        out_specs=(vm, vm, vm),
+        scratch_shapes=[
+            pltpu.VMEM((16, 32, 896), bf),
+            pltpu.VMEM((16, 32, 896), bf),
+            pltpu.VMEM((32, 896), f32),
+            pltpu.VMEM((32, 896), f32),
+            pltpu.VMEM((32, 896), bf),
+            pltpu.VMEM((4, 2, 4, 2, 2, 32, 1024), bf),
+            pltpu.VMEM((512, 7168), bf),
+            pltpu.VMEM((512, 512), f32),
+            pltpu.VMEM((16, 128), f32),
+            pltpu.VMEM((8, 16, 128), f32),
+            pltpu.VMEM((16, 16, 128), f32),
+            dma, dma((16,)), dma((16,)), dma((2,)), dma((2,)), dma((9,)), dma((9,)), dma((9,)), dma((9,)),
+            dma((18,)), dma((18,)), dma((12,)), dma((12,)), dma((8,)), dma((8,)), dma((16,)), dma((16,)),
+        ],
+        compiler_params=pltpu.CompilerParams(collective_id=2, has_side_effects=True, vmem_limit_bytes=50 << 20),
+        cost_estimate=pl.CostEstimate(flops=5_000_000_000, bytes_accessed=22_000_000, transcendentals=300_000),
+        name="head",
+    )(rows, proj, resid, gain, lm_head, table, accept)
 
 
 def body(
@@ -355,9 +601,7 @@
     cache_len,
     accept_len,
 ):
-    requests, draft_count, local_heads, nope_width = q_nope.shape
-    score_scale = 1.0 / math.sqrt(nope_width + q_rope.shape[3])
-    seq_index = lax.axis_index(SEQ)
+    score_scale = 1.0 / math.sqrt(q_nope.shape[3] + q_rope.shape[3])
     batch_index = lax.axis_index(BATCH)
     bf = jnp.bfloat16
     latent = jnp.einsum("ihn,hnc->hic", q_nope[0], absorb_k, preferred_element_type=jnp.float32)
@@ -367,55 +611,14 @@
     draft = jnp.pad(jnp.concatenate([draft_latent[0], draft_rope[0]], axis=1), ((0, 64), (0, 64)))
     own_parent = lax.dynamic_slice_in_dim(parent, batch_index, 1, 0)[0]
     parent_col = jnp.broadcast_to(jnp.pad(own_parent, (0, 64))[:, None], (128, 128))
+    odd = lax.rem(lax.axis_index("seq_1"), 2) == 1
+    resid = jnp.where(odd, jnp.pad(residual, ((0, 0), (448, 0))), jnp.pad(residual, ((0, 0), (0, 448))))
+    table = jnp.concatenate([parent.reshape(4, 128), draft_ids.reshape(4, 128)], axis=0).astype(jnp.float32)
     head_rows = attention(query, cache_latent[0], kr, draft, parent_col, absorb_v, cache_len, score_scale)
-    branch_term = jnp.dot(head_rows, out_proj, preferred_element_type=jnp.float32)
-    width_local = residual.shape[1]
-    feature_first = seq_index * width_local
-    residual_wide = lax.dynamic_update_slice_in_dim(
-        jnp.zeros_like(branch_term), residual.astype(jnp.float32), feature_first, 1
-    )
-    stream = lax.psum(branch_term + residual_wide, SEQ)
-    square = jnp.sum(stream * stream, axis=1)
-    normed = (
-        stream * lax.rsqrt(square / stream.shape[1] + norm_epsilon)[:, None] * norm_gain
-    ).astype(jnp.bfloat16)
-    hidden_out = lax.dynamic_slice_in_dim(stream, feature_first, width_local, 1).astype(
-        jnp.bfloat16
-    )
-    vocab_rows = lm_head.shape[0]
-    vocab_first = lax.axis_index(SEQ_BATCH) * vocab_rows
-    logits = jnp.einsum(
-        "rd,vd->rv",
-        lax.all_gather(normed, BATCH, axis=0, tiled=True),
-        lm_head,
-        preferred_element_type=jnp.float32,
-    )
-    request_total = parent.shape[0]
-    parent_rows = (
-        jnp.arange(request_total, dtype=jnp.int32)[:, None] * draft_count + parent
-    ).reshape(-1)
-    source = logits[parent_rows]
-    column = jnp.arange(vocab_rows, dtype=jnp.int32) + vocab_first
-    picked = jnp.sum(
-        jnp.where(column[None, :] == draft_ids.reshape(-1)[:, None], source, 0.0), axis=1
-    )
-    local_best = jnp.max(logits, axis=1)
-    local_mass = jnp.sum(jnp.exp(logits - local_best[:, None]), axis=1)
-    best, exp_mass, chosen = combined_by_axis(
-        (local_best, local_mass, picked), SEQ_BATCH, combine_soft
-    )
-    log_total = best + jnp.log(exp_mass)
-    target_all = (chosen - log_total[parent_rows]).reshape(request_total, draft_count)
-    target_logp = lax.dynamic_slice_in_dim(target_all, batch_index * requests, requests, 0)
-    accepted_score = jnp.sum(
-        jnp.where(
-            jnp.arange(draft_count, dtype=jnp.int32)[None, :] < accept_len[:, None],
-            target_logp,
-            0.0,
-        ),
-        axis=1,
-    )
-    return (hidden_out, target_logp, accepted_score)
+    hidden, target, score = head(head_rows, out_proj, resid, norm_gain[None], lm_head, table, accept_len)
+    hidden = hidden.reshape(64, 896)
+    hidden_out = jnp.where(odd, hidden[:, 448:], hidden[:, :448])
+    return (hidden_out, target[:1, :64], score[0, :1])
 
 
 def solution(mesh):

time: 294 us -> 155 us (0.53)
  waiting for transfers between devices: 137 us -> 0 us
  Pallas kernels: 73 us -> 146 us
  blocking collectives: 38.3 us -> 0 us
  between operations: 15.8 us -> 2.2 us
  matrix products: 12.3 us -> 1.24 us
  local copies, waits for them, and re-layouts: 12 us -> 4.46 us
  other arithmetic: 5.12 us -> 0.92 us
    psum x1 -> x0, waiting for transfers between devices: 92.3 us -> none  [body(): stream = lax.psum(branch_term + residual_wide, SEQ)]
    pallas_call x0 -> x1, Pallas kernels: none -> 73.5 us  [head(): pl.pallas_call(head_kernel, out_shape=(jax.ShapeDtypeStruct((2, 32, 896),...]
    all_gather x1 -> x0, waiting for transfers between devices: 44.7 us -> none  [body(): lax.all_gather(normed, BATCH, axis=0, tiled=True)]
    all_gather x4 -> x0, blocking collectives: 38.3 us -> none  [gathered_once(): both, at, found = (lax.all_gather(jnp.concatenate(lines), axis), 0, {})]
    dot_general x2 -> x0, matrix products: 11.1 us -> none  [the longest x1 8.44 us: body(): jnp.einsum('rd,vd->rv', lax.all_gather(normed, BATCH, axis=0, tiled=True)...]
    gather x3 -> x0, local copies, waits for them, and re-layouts: 5.18 us -> none  [the longest x2 3.57 us: body(): log_total[parent_rows]]
    reduce_sum x4 -> x0, other arithmetic: 3.42 us -> none  [the longest x1 1.85 us: body(): square = jnp.sum(stream * stream, axis=1)]
  transfers between devices with their start and end apart: 2 -> 0, of which waited for: 2 -> 0; matrix products, arithmetic and copies ran while one was open for 0% -> 0% of each run, Pallas kernels for 0% -> 0%
where the time goes in v2:
time: 155 us
  Pallas kernels  146 us (94%)
  local copies, waits for them, and re-layouts  4.46 us (3%)
  between operations  2.2 us (1%)
    pallas_call x1, Pallas kernels, head(): pl.pallas_call(head_kernel, out_shape=(jax.ShapeDtypeStruct((2, 32, 896),...  73.5 us
    pallas_call x1, Pallas kernels, attention(): pl.pallas_call(functools.partial(attention_kernel, scale * math.log2(math...  72.8 us

profile of v2, /device:TPU:1, one launch (start us, length us, event | category | flops | bytes accessed | tf_op | source)
XLA Modules:
  0.0 155.1 jit_solution(9533601489317571599)
XLA Ops:
  0.6 0.0 copy-start
  1.4 0.9 copy.32
  2.3 0.0 copy-done
  2.3 0.0 copy-start.4
  2.3 1.2 convolution_convert_fusion
  3.6 0.0 copy-start.5
  3.6 0.0 copy-start.7
  3.6 0.0 copy-start.9
  3.6 0.0 copy-start.2
  3.6 0.1 fusion.1
  3.7 0.0 copy-done.4
  3.7 0.1 reshape_squeeze.3
  3.8 0.1 copy.28.kr_ref
  3.9 0.5 copy-done.5
  4.4 0.0 copy-done.7
  4.4 0.0 copy-done.9
  4.5 0.1 broadcast_in_dim.4.parent_ref
  4.6 0.3 copy-done.2
  4.9 0.0 copy-start.3
  4.9 1.2 copy-done.3
  6.1 0.0 copy-start.6
  6.1 0.0 copy-start.8
  6.1 0.0 copy-start.1
  6.1 72.8 %attention.1.rows_ref = bf16[64,1024]{1,0:T(8,128)(2,1)S(1)} custom-call(s32[1]{0:T(128)S(6)} %copy.33.len_ref, bf16[512,640]{1,0:T(8,128)(2,1)S(1)} %bitcast.20, bf16[1024,512]{1,0:T(8,128)(2,1)S(1)} %bitcast.23, bf16[2,256,128]{2,1,0:T(8,128)(2,1)S(1)} %copy.28.kr_ref, bf16[128,640]{1,0:T(8,128)(2,1)S(1)} %fusion.7.draft_ref, ...), custom_call_target="tpu_custom_call" | custom-call | flops 20000000000 | bytes 20000000 | tf_op jit(solution)/shard_map/attention/pallas_call | solution.py:243
  78.9 0.0 copy-done.6
  78.9 0.1 pad_select_fusion.resid_ref
  79.0 0.0 copy-done.8
  79.0 0.1 reshape.25
  79.1 0.1 reshape.24
  79.9 0.0 copy-done.1
  79.9 73.5 %head.1 = (bf16[2,32,896]{2,1,0:T(8,128)(2,1)S(1)}, f32[8,128]{1,0:T(8,128)S(1)}, f32[8,128]{1,0:T(8,128)S(1)}) custom-call(bf16[64,1024]{1,0:T(8,128)(2,1)S(1)} %attention.1.rows_ref, bf16[1024,7168]{1,0:T(8,128)(2,1)} %proj_ref.1, bf16[64,896]{1,0:T(8,128)(2,1)S(1)} %pad_select_fusion.resid_ref, f32[1,7168]{1,0:T(1,128)S(1)} %bitcast.22, ...), custom_call_target="tpu_custom_call" | custom-call | flops 5000000000 | bytes 22000000 | tf_op jit(solution)/shard_map/head/pallas_call | solution.py:556
  153.4 0.7 slice_select_fusion
  154.1 0.5 slice.14
  154.6 0.5 slice.15
  (5 shorter events, 0.1 us)
Async XLA Ops:
  0.6 1.7 %copy-start = (bf16[8,128,512]{2,1,0:T(8,128)(2,1)S(1)}, bf16[8,128,512]{2,1,0:T(8,128)(2,1)}, u32[]{:S(2)}) copy-start(bf16[8,128,512]{2,1,0:T(8,128)(2,1)} %param.18) | copy-start | bytes 3145732
  2.3 1.4 copy-start.4
  3.6 0.8 copy-start.5
  3.6 0.8 copy-start.7
  3.6 0.8 copy-start.9
  3.6 1.3 copy-start.2
  4.9 1.2 copy-start.3
  6.1 72.8 %copy-start.6 = (bf16[64,448]{1,0:T(8,128)(2,1)S(1)}, bf16[64,448]{1,0:T(8,128)(2,1)}, u32[]{:S(2)}) copy-start(bf16[64,448]{1,0:T(8,128)(2,1)} %param.24) | copy-start | bytes 172036
  6.1 72.9 %copy-start.8 = (s32[8,64]{1,0:T(8,128)S(1)}, s32[8,64]{1,0:T(8,128)}, u32[]{:S(2)}) copy-start(s32[8,64]{1,0:T(8,128)} %param.29) | copy-start | bytes 6148
  6.1 73.8 %copy-start.1 = (f32[7168]{0:T(1024)S(1)}, f32[7168]{0:T(1024)}, u32[]{:S(2)}) copy-start(f32[7168]{0:T(1024)} %param.26) | copy-start | bytes 86020

commit v3 on v1

v3 whole, which is shorter than its diff:
```python
import functools
import math

import jax
import jax.numpy as jnp
from jax import lax
from jax.experimental import pallas as pl
from jax.experimental.pallas import tpu as pltpu
from jax.sharding import Mesh
from jax.sharding import PartitionSpec as P

SEQ = ("seq_0", "seq_1")
BATCH = ("batch_0", "batch_1")
SEQ_BATCH = ("seq_0", "seq_1", "batch_0", "batch_1")

norm_epsilon = 1e-06
MESH_ID = pl.DeviceIdType.MESH
LOWEST = -1e28
MASKED = -1e30
TRANS_B = (((1,), (1,)), ((), ()))


def whole_kernel(scale, len_ref, accept_ref, nope_ref, rope_ref, ak_ref, kl_ref, kr_ref, dl_ref, dr_ref, parent_ref, ids_ref,
                 av_ref, proj_ref, resid_ref, gain_ref, lm_ref, hid_ref, target_ref, score_ref,
                 qbuf, kbuf, krbuf, avbuf, acc, top, mass, part, part_in, stat, stat_in, lse, tree, names, rows_ref,
                 proj, lm, out_part, out_in, near, near_in, padded, hid_own, hid_in, wide, logits, rates, tiles, merged, tile1, tile2,
                 loc_sem, q_send, q_recv, k_send, k_recv, r_send, r_recv, v_send, v_recv, p_send, p_recv,
                 s_send, s_recv, n_sem, h_sem, g1_send, g1_recv, g2_send, g2_recv, g3_send, g3_recv,
                 c_send, c_recv, f1_send, f1_recv, f2_send, f2_recv):
    y, z = lax.axis_index("seq_0"), lax.axis_index("seq_1")
    x, c = lax.axis_index("batch_0"), lax.axis_index("batch_1")
    zh, zl = z // 2, lax.rem(z, 2)
    me, group, place = y * 4 + z, y * 2 + z // 2, x * 2 + c
    bf, f32 = jnp.bfloat16, jnp.float32
    turn = lambda at, by: lax.rem(at + by, 4)

    def seq_peer(s):
        return {"seq_0": s // 4, "seq_1": lax.rem(s, 4)}

    def batch_peer(b):
        return {"batch_0": b // 2, "batch_1": lax.rem(b, 2)}

    barrier = pltpu.get_barrier_semaphore()

    def greet_seq(k, _):
        pl.semaphore_signal(barrier, inc=1, device_id=seq_peer(lax.rem(me + k, 16)), device_id_type=MESH_ID)
        return 0

    def greet_batch(k, _):
        pl.semaphore_signal(barrier, inc=1, device_id=batch_peer(lax.rem(place + k, 8)), device_id_type=MESH_ID)
        return 0

    lax.fori_loop(1, 16, greet_seq, 0)
    lax.fori_loop(1, 8, greet_batch, 0)

    def describe(src, dst, send, recv, peer):
        return pltpu.make_async_remote_copy(src_ref=src, dst_ref=dst, send_sem=send, recv_sem=recv,
                                            device_id=peer, device_id_type=MESH_ID)

    def remote(*spec):
        copy = describe(*spec)
        copy.start()
        return copy

    def local_copy(src, dst, n):
        copy = pltpu.make_async_copy(src, dst, loc_sem.at[n])
        copy.start()
        return copy

    local = []
    for h in range(2):
        local.append(local_copy(kl_ref.at[pl.ds(512 * h, 512)], kbuf.at[h], h))
        local.append(local_copy(kr_ref.at[:, pl.ds(512 * h, 512)], krbuf.at[h, pl.ds(0, 64)], 2 + h))
    local_av = local_copy(av_ref, avbuf.at[0], 4)
    pl.semaphore_wait(barrier, 22)
    y_right, y_left, y_far = {"seq_0": turn(y, 1)}, {"seq_0": turn(y, 3)}, {"seq_0": turn(y, 2)}
    z_right, z_left = {"seq_1": turn(z, 1)}, {"seq_1": turn(z, 3)}
    sibling = {"batch_1": 1 - c}
    half = lambda h: pl.ds(256 * h, 256)
    sends = []
    q_in, k_in, r_in = {}, {}, {}
    for slot, peer, order in ((1, z_right, (0, 1)), (2, z_left, (1, 0))):
        for h in order:
            n = slot * 2 + h
            k_in[n] = remote(kl_ref.at[pl.ds(512 * h, 512)], kbuf.at[n], k_send.at[n], k_recv.at[n], peer)
            r_in[n] = remote(kr_ref.at[:, pl.ds(512 * h, 512)], krbuf.at[n, pl.ds(0, 64)], r_send.at[n], r_recv.at[n], peer)

    content = jnp.swapaxes(nope_ref[...].astype(f32), 0, 1).astype(bf)
    rotary = jnp.swapaxes(rope_ref[...].astype(f32), 0, 1).astype(bf)
    for h in range(8):
        rows = slice(64 * h, 64 * h + 64)
        qbuf[0, rows, 0:512] = jnp.dot(content[h], ak_ref[h], preferred_element_type=f32).astype(bf)
        qbuf[0, rows, 512:576] = rotary[h]
        qbuf[0, rows, 576:640] = jnp.zeros((64, 64), bf)
    for slot, peer, order in ((1, y_right, (0, 1)), (2, y_left, (1, 0))):
        for h in order:
            n = slot * 2 + h
            q_in[n] = remote(qbuf.at[0, half(h)], qbuf.at[slot, half(h)], q_send.at[n], q_recv.at[n], peer)
    proj_copy = local_copy(proj_ref, proj, 5)
    lm_copy = local_copy(lm_ref, lm, 6)
    acc[...] = jnp.zeros_like(acc)
    top[...] = jnp.full(top.shape, LOWEST, f32)
    mass[...] = jnp.zeros_like(mass)

    names[...] = jnp.zeros_like(names)
    names[0:8, 0:64] = parent_ref[...].astype(f32)
    names[8:16, 0:64] = ids_ref[...].astype(f32)
    own_line = lax.broadcasted_iota(jnp.int32, (8, 128), 0) == place
    own_parents = jnp.sum(jnp.where(own_line, names[0:8], 0.0), axis=0, keepdims=True)
    own_parents = jnp.transpose(jnp.broadcast_to(own_parents, (128, 128))).astype(jnp.int32)
    tree[...] = jnp.zeros_like(tree)
    tree[0:64, 0:512] = dl_ref[...]
    tree[0:64, 512:576] = dr_ref[...]
    for n in range(8):
        krbuf[n, 64:128] = jnp.zeros((64, 512), bf)
    row = lax.broadcasted_iota(jnp.int32, (128, 128), 0)
    col = lax.broadcasted_iota(jnp.int32, (128, 128), 1)
    hop = ((own_parents == col) & (row > 0) & (row < 64)).astype(f32)
    known = (row == col).astype(f32)
    for _ in range(6):
        step = hop.astype(bf)
        known = known + jnp.dot(known.astype(bf), step, preferred_element_type=f32)
        hop = jnp.dot(step, step, preferred_element_type=f32)
    tree_bias = jnp.where((known > 0.5) & (col < 64), 0.0, MASKED)[:64]

    def update(slot, rows, count, find, values, bias):
        width = bias.shape[1]
        at = (slot, pl.ds(rows, count))
        scores = find(qbuf[at]) * scale + bias
        before = top[at]
        now = jnp.maximum(before, jnp.max(scores, axis=1, keepdims=True))
        weights = jnp.exp2(scores - jnp.tile(now, (1, width // 128)))
        fade = jnp.exp2(before - now)
        total = mass[at] * fade
        for k in range(width // 128):
            total = total + weights[:, 128 * k : 128 * k + 128]
        mass[at] = total
        top[at] = now
        acc[at] = acc[at] * jnp.tile(fade, (1, 4)) + jnp.dot(
            weights.astype(bf), values, preferred_element_type=f32
        )

    def tree_scores(query):
        return lax.dot_general(query, tree[...], TRANS_B, preferred_element_type=f32)

    for h in range(8):
        update(0, 64 * h, 64, tree_scores, tree[:, :512], tree_bias)

    def chunks(first, count, slots):
        def chunk(kc, _):
            turn_by = jnp.where(kc // 2 == 0, 0, jnp.where(kc // 2 == 1, 3, jnp.where(kc // 2 == 2, 1, 2)))
            start = (y * 4 + lax.rem(z + turn_by, 4)) * 1024 + lax.rem(kc, 2) * 512
            spot = start + lax.broadcasted_iota(jnp.int32, (1, 512), 1)
            bias = jnp.where(spot < len_ref[0], 0.0, MASKED)
            def cache_scores(query):
                return lax.dot_general(query[:, :512], kbuf[kc], TRANS_B, preferred_element_type=f32) + jnp.dot(
                    query[:, 512:], krbuf[kc], preferred_element_type=f32
                )

            for slot in slots:
                update(slot, 0, 512, cache_scores, kbuf[kc], bias)
            return 0

        lax.fori_loop(first, first + count, chunk, 0)

    for copy in local:
        copy.wait()
    chunks(0, 2, (0,))

    q_in[2].wait_recv()
    q_in[6] = remote(qbuf.at[1, half(0)], qbuf.at[3, half(0)], q_send.at[6], q_recv.at[6], y_right)
    q_in[5].wait_recv()
    q_in[7] = remote(qbuf.at[2, half(1)], qbuf.at[3, half(1)], q_send.at[7], q_recv.at[7], y_left)
    q_in[3].wait_recv()
    q_in[4].wait_recv()
    chunks(0, 2, (1, 2))

    def key_wait(n):
        k_in[n].wait_recv()
        r_in[n].wait_recv()

    def key_on(n, m, peer):
        k_in[m] = remote(kbuf.at[n], kbuf.at[m], k_send.at[m], k_recv.at[m], peer)
        r_in[m] = remote(krbuf.at[n, pl.ds(0, 64)], krbuf.at[m, pl.ds(0, 64)], r_send.at[m], r_recv.at[m], peer)

    key_wait(2)
    key_on(2, 6, z_right)
    key_wait(5)
    key_on(5, 7, z_left)
    chunks(2, 1, (0, 1, 2))
    chunks(5, 1, (0, 1, 2))
    q_in[6].wait_recv()
    q_in[7].wait_recv()
    v_in = {}
    mine = 4 * c
    pair = lambda first, h: pl.ds(first + 2 * h, 2)
    for slot, peer, order in ((1, y_right, (0, 1)), (2, y_left, (1, 0))):
        for h in order:
            n = slot * 2 + h
            v_in[n] = remote(av_ref.at[pair(mine, h)], avbuf.at[slot, pair(mine, h)], v_send.at[n], v_recv.at[n], peer)
    chunks(0, 3, (3,))
    chunks(5, 1, (3,))
    v_in[2].wait_recv()
    v_in[6] = remote(avbuf.at[1, pair(mine, 0)], avbuf.at[3, pair(mine, 0)], v_send.at[6], v_recv.at[6], y_right)
    v_in[5].wait_recv()
    v_in[7] = remote(avbuf.at[2, pair(mine, 1)], avbuf.at[3, pair(mine, 1)], v_send.at[7], v_recv.at[7], y_left)
    key_wait(3)
    key_wait(4)
    chunks(3, 2, (0, 1, 2, 3))
    v_in[3].wait_recv()
    v_in[4].wait_recv()
    v_over = {}
    for slot in (1, 2):
        v_over[slot] = remote(avbuf.at[slot, pl.ds(mine, 4)], avbuf.at[slot, pl.ds(mine, 4)], v_send.at[7 + slot], v_recv.at[7 + slot], sibling)
    v_in[6].wait_recv()
    v_in[7].wait_recv()
    v_over[3] = remote(avbuf.at[3, pl.ds(mine, 4)], avbuf.at[3, pl.ds(mine, 4)], v_send.at[10], v_recv.at[10], sibling)
    key_wait(6)
    key_wait(7)
    local_av.wait()
    for slot in (1, 2, 3):
        v_over[slot].wait_recv()

    def finish(slot):
        for h in range(8):
            at = (slot, slice(64 * h, 64 * h + 64))
            total = jnp.sum(mass[at], axis=1, keepdims=True)
            some = total > 0.0
            safe = jnp.where(some, total, 1.0)
            value = jnp.dot(acc[at].astype(bf), avbuf[slot, h], preferred_element_type=f32)
            part[at] = (value * jnp.where(some, 1.0 / safe, 0.0)).astype(bf)
            lse[64 * h : 64 * h + 64] = jnp.where(some, top[at] + jnp.log2(safe), LOWEST)
        for k in range(4):
            stat[slot, pl.ds(k, 1)] = jnp.transpose(lse[pl.ds(128 * k, 128)])[:1]

    p_in = []
    for slot, landing, peer in ((3, 3, y_far), (1, 2, y_left), (2, 1, y_right)):
        chunks(6, 2, (slot,))
        finish(slot)
        p_in.append(remote(part.at[slot], part_in.at[landing], p_send.at[landing], p_recv.at[landing], peer))
        p_in.append(remote(stat.at[slot], stat_in.at[landing], p_send.at[landing + 4], p_recv.at[landing + 4], peer))
    chunks(6, 2, (0,))
    finish(0)
    for copy in p_in:
        copy.wait_recv()
    levels = [stat[0, :4]] + [stat_in[k, :4] for k in (1, 2, 3)]
    best = jnp.maximum(jnp.maximum(levels[0], levels[1]), jnp.maximum(levels[2], levels[3]))
    shares = [jnp.exp2(level - best) for level in levels]
    whole = 1.0 / (shares[0] + shares[1] + shares[2] + shares[3])
    for k in range(4):
        rows = pl.ds(128 * k, 128)
        mixed = jnp.zeros((128, 128), f32)
        for j in range(4):
            share = jnp.transpose(jnp.broadcast_to((shares[j] * whole)[k : k + 1], (128, 128)))
            block = part[0, rows] if j == 0 else part_in[j, rows]
            mixed = mixed + share * block.astype(f32)
        mixed = mixed.astype(bf)
        rows_ref[:, pl.ds(256 * k, 128)] = mixed[:64]
        rows_ref[:, pl.ds(256 * k + 128, 128)] = mixed[64:]

    def product(g):
        return jnp.dot(rows_ref[...], proj[:, pl.ds(pl.multiple_of(g * 896, 128), 896)], preferred_element_type=f32)

    def outward(s):
        return describe(out_part.at[s], out_in.at[me], s_send.at[s], s_recv.at[me], seq_peer(s))

    def inward(s):
        return describe(out_part.at[s], out_in.at[s], s_send.at[s], s_recv.at[s], seq_peer(s))

    def make(g):
        block = product(g).astype(bf)
        out_part[2 * g] = block[:32]
        out_part[2 * g + 1] = block[32:]

    proj_copy.wait()
    make(lax.rem(group + 1, 8))

    def spread(k, _):
        g = lax.rem(group + k, 8)
        outward(2 * g).start()
        outward(2 * g + 1).start()

        @pl.when(k < 7)
        def _():
            make(lax.rem(group + k + 1, 8))

        return 0

    lax.fori_loop(1, 8, spread, 0)
    padded[...] = jnp.zeros_like(padded)
    for side in range(2):

        @pl.when(zl == side)
        def _():
            padded[:, 448 * side : 448 * side + 448] = resid_ref[...].astype(f32)

    mine = product(group) + padded[...]
    first = zl == 0
    near[...] = jnp.where(first, mine[32:], mine[:32])
    partner = {"seq_1": zh * 2 + 1 - zl}
    near_copy = remote(near, near_in, n_sem.at[0], n_sem.at[1], partner)
    stream = jnp.where(first, mine[:32], mine[32:])
    other = group * 2

    def collect(k, total):
        s = lax.rem(other + 1 + k, 16)
        inward(s).wait_recv()
        return total + out_in[s].astype(f32)

    stream = lax.fori_loop(1, 15, collect, stream)
    near_copy.wait_recv()
    stream = stream + near_in[...]

    squares = jnp.sum(stream * stream, axis=1, keepdims=True)
    high = squares.astype(bf)
    low = (squares - high.astype(f32)).astype(bf)
    lane = lax.broadcasted_iota(jnp.int32, (32, 128), 1)
    at = (y, zh, x, c, zl)
    wide[(*at, slice(None), pl.ds(0, 896))] = (stream * gain_ref[:, pl.ds(pl.multiple_of(group * 896, 128), 896)]).astype(bf)
    wide[(*at, slice(None), pl.ds(896, 128))] = jnp.where(lane < 64, high.astype(f32), low.astype(f32)).astype(bf)

    lanes = (pl.ds(0, 384), pl.ds(384, 384), pl.ds(768, 256))
    every = slice(None)
    along = {"x": ("batch_0", x), "y": ("seq_0", y), "z": ("seq_1", z)}

    def turned(axis, by):
        name, own = along[axis]
        return {name: lax.rem(own + by, 4)}

    def view(p, done, pos, half=None):
        py, pz, px = pos["y"], pos["z"], pos["x"]
        iy = every if "y" in done else py
        izh, izl = (every, every) if "z" in done else (pz // 2, lax.rem(pz, 2))
        ix = every if "x" in done else px
        if half is not None:
            if "y" in done:
                iy = pl.ds(2 * half, 2)
            else:
                izh = pl.ds(half, 1)
        return wide.at[iy, izh, ix, pos.get("c", c), izl, :, lanes[p]]

    orders = (("x", "y", "z"), ("y", "z", "x"), ("z", "x", "y"))
    here = {"x": x, "y": y, "z": z}

    def moved(axis, by):
        return {**here, axis: lax.rem(here[axis] + by, 4)}

    pending = []
    hid_own[...] = stream.astype(bf)
    hid_copy = None
    waits = {}
    for stage, (sends, recvs) in enumerate(((g1_send, g1_recv), (g2_send, g2_recv))):
        for p in range(3):
            axis, done = orders[p][stage], orders[p][:stage]
            for k in (1, 3, 2):
                n = p * 3 + k - 1
                own = view(p, done, here)
                copy = remote(own, own, sends.at[n], recvs.at[n], turned(axis, k))
                pending.append(copy)
                waits[stage, p, k] = (done, axis, n, sends, recvs)
        if stage == 0:
            hid_copy = remote(hid_own, hid_in.at[zl], h_sem.at[0], h_sem.at[1], partner)
            hid_in[zl] = hid_own[...]
        for p in range(3):
            done, axis = orders[p][:stage], orders[p][stage]
            for k in (1, 3, 2):
                n = p * 3 + k - 1
                came = view(p, done, moved(axis, 4 - k))
                describe(came, came, sends.at[n], recvs.at[n], turned(axis, k)).wait_recv()
    sibling = {"batch_1": 1 - c}

    def over(p, n, which):
        copy = remote(which, which, c_send.at[n], c_recv.at[n], sibling)
        pending.append(copy)

    for p in range(3):
        axis, done = orders[p][2], orders[p][:2]
        for k, halves in ((1, (0, 1)), (3, (1, 0))):
            for half in halves:
                n = p * 6 + (k // 2) * 2 + half
                own = view(p, done, here, half)
                pending.append(remote(own, own, g3_send.at[n], g3_recv.at[n], turned(axis, k)))
    for p in range(3):
        over(p, p * 4, view(p, orders[p][:2], here))

    def came3(p, k, half):
        axis, done = orders[p][2], orders[p][:2]
        n = p * 6 + {1: 0, 3: 2, 2: 4}[k] + half
        block = view(p, done, moved(axis, 4 - k), half)
        describe(block, block, g3_send.at[n], g3_recv.at[n], turned(axis, 1)).wait_recv()
        return block

    for p in range(3):
        axis = orders[p][2]
        block = came3(p, 1, 0)
        pending.append(remote(block, block, g3_send.at[p * 6 + 4], g3_recv.at[p * 6 + 4], turned(axis, 1)))
        block = came3(p, 3, 1)
        pending.append(remote(block, block, g3_send.at[p * 6 + 5], g3_recv.at[p * 6 + 5], turned(axis, 3)))
    for p in range(3):
        axis, done = orders[p][2], orders[p][:2]
        came3(p, 1, 1)
        over(p, p * 4 + 1, view(p, done, moved(axis, 3)))
        came3(p, 3, 0)
        over(p, p * 4 + 2, view(p, done, moved(axis, 1)))
    for p in range(3):
        axis, done = orders[p][2], orders[p][:2]
        came3(p, 2, 0)
        came3(p, 2, 1)
        over(p, p * 4 + 3, view(p, done, moved(axis, 2)))
    lm_copy.wait()

    def contract(core):
        logits[:, core] = jnp.zeros((4, 64, 512), f32)

        def step(g, squares):
            left = wide[g // 2, lax.rem(g, 2), :, core].reshape(256, 1024)
            right = lm[:, pl.ds(pl.multiple_of(g * 896, 128), 896)]
            added = lax.dot_general(left[:, :896], right, TRANS_B, preferred_element_type=f32)
            logits[:, core] += added.reshape(4, 64, 512)
            return squares + left[:, 896:].astype(f32)

        squares = lax.fori_loop(0, 8, step, jnp.zeros((256, 128), f32))
        rate = lax.rsqrt(jnp.sum(squares, axis=1, keepdims=True) * (1.0 / (64 * 7168)) + norm_epsilon)
        rates[:, core] = jnp.broadcast_to(rate, (256, 128)).reshape(4, 64, 128)

    contract(c)
    for p in range(3):
        axis, done = orders[p][2], orders[p][:2]
        for n, by in ((0, 0), (1, 3), (2, 1), (3, 2)):
            block = view(p, done, {**moved(axis, by), "c": 1 - c})
            describe(block, block, c_send.at[p * 4 + n], c_recv.at[p * 4 + n], sibling).wait_recv()
    contract(1 - c)
    vocab_first = (me * 8 + place) * 512
    entry = lax.broadcasted_iota(jnp.int32, (64, 512), 1) + vocab_first
    spot = lax.broadcasted_iota(jnp.int32, (64, 128), 1)
    tiles[...] = jnp.zeros_like(tiles)

    def column(r):
        return jnp.transpose(jnp.broadcast_to(names[r : r + 1], (128, 128)))[:64].astype(jnp.int32)

    for k in range(4):
        found = [[], [], []]
        for h in range(2):
            parents, wanted = column(2 * k + h), column(8 + 2 * k + h)
            values = logits[k, h] * jnp.tile(rates[k, h], (1, 4))
            best = jnp.max(values, axis=1, keepdims=True)
            mass_here = jnp.sum(jnp.exp(values - best), axis=1, keepdims=True)
            choose = (parents == spot).astype(bf)[:, :64]
            rest, source = values, jnp.zeros((64, 512), f32)
            for _ in range(3):
                piece = rest.astype(bf)
                source = source + jnp.dot(choose, piece, preferred_element_type=f32)
                rest = rest - piece.astype(f32)
            hit = entry == jnp.tile(wanted, (1, 4))
            pick = jnp.sum(jnp.where(hit, source, 0.0), axis=1, keepdims=True)
            for i, one in enumerate((best, mass_here, pick)):
                found[i].append(jnp.broadcast_to(one, (64, 128)))
        for i in range(3):
            line = jnp.transpose(jnp.concatenate(found[i], axis=0))[:8]
            tiles[2 * k, i : i + 1] = line[:1]
            tiles[2 * k + 1, i : i + 1] = pltpu.roll(line, 64, 1)[:1]

    def merge(blocks):
        best = functools.reduce(jnp.maximum, [b[0:1] for b in blocks])
        total = sum(b[1:2] * jnp.exp(b[0:1] - best) for b in blocks)
        return best, total, sum(b[2:3] for b in blocks)

    for k in range(1, 8):
        b = lax.rem(place + k, 8)
        pending.append(remote(tiles.at[b], tile1.at[k], f1_send.at[k], f1_recv.at[k], batch_peer(b)))
    blocks = [tiles[place]]
    for k in range(1, 8):
        describe(tiles.at[0], tile1.at[k], f1_send.at[k], f1_recv.at[k], batch_peer(lax.rem(place + k, 8))).wait_recv()
        blocks.append(tile1[k])
    best, mass_here, pick = merge(blocks)
    merged[...] = jnp.zeros_like(merged)
    merged[0:1] = best
    merged[1:2] = mass_here
    merged[2:3] = pick
    for k in range(1, 16):
        pending.append(remote(merged, tile2.at[k], f2_send.at[k], f2_recv.at[k], seq_peer(lax.rem(me + k, 16))))
    blocks = [merged[...]]
    for k in range(1, 16):
        describe(merged, tile2.at[k], f2_send.at[k], f2_recv.at[k], seq_peer(lax.rem(me + k, 16))).wait_recv()
        blocks.append(tile2[k])
    best, mass_here, pick = merge(blocks)
    log_total = jnp.broadcast_to(best + jnp.log(mass_here), (128, 128))
    lane = lax.broadcasted_iota(jnp.int32, (128, 128), 1)
    own_parents = jnp.sum(jnp.where(own_line, names[0:8], 0.0), axis=0, keepdims=True)
    own_parents = jnp.transpose(jnp.broadcast_to(own_parents, (128, 128))).astype(jnp.int32)
    of_parent = jnp.sum(jnp.where((own_parents == lane) & (lane < 64), log_total, 0.0), axis=1, keepdims=True)
    of_parent = jnp.transpose(jnp.broadcast_to(of_parent, (128, 128)))[:8]
    target = jnp.broadcast_to(pick, (8, 128)) - of_parent
    target_ref[...] = target[:1, :64]
    kept = lane[:8] < jnp.minimum(accept_ref[0], 64)
    score_ref[...] = jnp.sum(jnp.where(kept, target, 0.0), axis=1, keepdims=True)[:1]

    hid_back = describe(hid_own, hid_in.at[1 - zl], h_sem.at[0], h_sem.at[1], partner)
    hid_back.wait_recv()
    for side in range(2):

        @pl.when(zl == side)
        def _():
            for h in range(2):
                hid_ref[32 * h : 32 * h + 32] = hid_in[h, :, 448 * side : 448 * side + 448]

    hid_copy.wait_send()
    near_copy.wait_send()

    def sent(k, _):
        outward(lax.rem(other + 1 + k, 16)).wait_send()
        return 0

    lax.fori_loop(1, 15, sent, 0)
    for copy in pending:
        copy.wait_send()
    for table in (q_in, k_in, r_in, v_in, v_over):
        for copy in table.values():
            copy.wait_send()
    for copy in p_in:
        copy.wait_send()


def whole(scale, cache_len, accept, nope, rope, absorb_k, kl, kr, dl, dr, parent, ids, absorb_v, proj, resid, gain, lm_head):
    bf, f32 = jnp.bfloat16, jnp.float32
    vm, hbm, sm = (pl.BlockSpec(memory_space=space) for space in (pltpu.VMEM, pl.ANY, pltpu.SMEM))
    dma, vmem = pltpu.SemaphoreType.DMA, pltpu.VMEM
    return pl.pallas_call(
        functools.partial(whole_kernel, scale * math.log2(math.e)),
        out_shape=(
            jax.ShapeDtypeStruct((64, 448), bf),
            jax.ShapeDtypeStruct((1, 64), f32),
            jax.ShapeDtypeStruct((1, 1), f32),
        ),
        in_specs=[sm, sm, vm, vm, vm, hbm, hbm, vm, vm, vm, vm, hbm, hbm, vm, vm, hbm],
        out_specs=(vm, vm, vm),
        scratch_shapes=[
            vmem((4, 512, 640), bf), vmem((8, 512, 512), bf), vmem((8, 128, 512), bf), vmem((4, 8, 512, 128), bf),
            vmem((4, 512, 512), f32), vmem((4, 512, 128), f32), vmem((4, 512, 128), f32),
            vmem((4, 512, 128), bf), vmem((4, 512, 128), bf), vmem((4, 8, 128), f32), vmem((4, 8, 128), f32),
            vmem((512, 128), f32), vmem((128, 640), bf), vmem((16, 128), f32), vmem((64, 1024), bf),
            vmem((1024, 7168), bf), vmem((512, 7168), bf), vmem((16, 32, 896), bf), vmem((16, 32, 896), bf),
            vmem((32, 896), f32), vmem((32, 896), f32), vmem((64, 896), f32), vmem((32, 896), bf), vmem((2, 32, 896), bf),
            vmem((4, 2, 4, 2, 2, 32, 1024), bf),
            vmem((4, 2, 64, 512), f32), vmem((4, 2, 64, 128), f32), vmem((8, 8, 128), f32), vmem((8, 128), f32),
            vmem((8, 8, 128), f32), vmem((16, 8, 128), f32),
            dma((7,)), dma((8,)), dma((8,)), dma((8,)), dma((8,)), dma((8,)), dma((8,)),
            dma((11,)), dma((11,)), dma((8,)), dma((8,)),
            dma((16,)), dma((16,)), dma((2,)), dma((2,)), dma((9,)), dma((9,)), dma((9,)), dma((9,)),
            dma((18,)), dma((18,)), dma((12,)), dma((12,)), dma((8,)), dma((8,)), dma((16,)), dma((16,)),
        ],
        compiler_params=pltpu.CompilerParams(collective_id=1, has_side_effects=True, vmem_limit_bytes=57 << 20),
        name="whole",
    )(cache_len, accept, nope, rope, absorb_k, kl, kr, dl, dr, parent, ids, absorb_v, proj, resid, gain, lm_head)


def body(
    q_nope,
    q_rope,
    absorb_k,
    absorb_v,
    cache_latent,
    cache_rope,
    draft_latent,
    draft_rope,
    residual,
    out_proj,
    norm_gain,
    lm_head,
    parent,
    draft_ids,
    cache_len,
    accept_len,
):
    score_scale = 1.0 / math.sqrt(q_nope.shape[3] + q_rope.shape[3])
    hidden, target, score = whole(
        score_scale, cache_len, accept_len, q_nope[0], q_rope[0], absorb_k, cache_latent[0], cache_rope[0].T,
        draft_latent[0], draft_rope[0], parent, draft_ids, absorb_v, out_proj, residual, norm_gain[None], lm_head,
    )
    return (hidden, target, score[0])


def solution(mesh):
    split = Mesh(mesh.devices.reshape(4, 4, 4, 2), ("seq_0", "seq_1", "batch_0", "batch_1"))
    in_specs = (
        P(BATCH, None, SEQ, None),
        P(BATCH, None, SEQ, None),
        P(SEQ, None, None),
        P(SEQ, None, None),
        P(BATCH, SEQ, None),
        P(BATCH, SEQ, None),
        P(BATCH, None, None),
        P(BATCH, None, None),
        P(BATCH, SEQ),
        P(SEQ, None),
        P(),
        P(SEQ_BATCH, None),
        P(),
        P(),
        P(BATCH),
        P(BATCH),
    )
    out_specs = (P(BATCH, SEQ), P(BATCH, None), P(BATCH))
    return jax.shard_map(body, mesh=split, in_specs=in_specs, out_specs=out_specs, check_vma=False)
```

time: 294 us -> 135 us (0.46)
  waiting for transfers between devices: 137 us -> 0 us
  Pallas kernels: 73 us -> 129 us
  blocking collectives: 38.3 us -> 0 us
  matrix products: 12.3 us -> 0 us
  between operations: 15.8 us -> 3.63 us
  local copies, waits for them, and re-layouts: 12 us -> 2.59 us
  other arithmetic: 5.12 us -> 0 us
    psum x1 -> x0, waiting for transfers between devices: 92.3 us -> none  [body(): stream = lax.psum(branch_term + residual_wide, SEQ)]
    pallas_call x1, Pallas kernels: 73 us -> 129 us  [whole(): pl.pallas_call(functools.partial(whole_kernel, scale * math.log2(math.e))...]
    all_gather x1 -> x0, waiting for transfers between devices: 44.7 us -> none  [body(): lax.all_gather(normed, BATCH, axis=0, tiled=True)]
    all_gather x4 -> x0, blocking collectives: 38.3 us -> none  [gathered_once(): both, at, found = (lax.all_gather(jnp.concatenate(lines), axis), 0, {})]
    dot_general x3 -> x0, matrix products: 12.3 us -> none  [the longest x1 8.44 us: body(): jnp.einsum('rd,vd->rv', lax.all_gather(normed, BATCH, axis=0, tiled=True)...]
    gather x3 -> x0, local copies, waits for them, and re-layouts: 5.18 us -> none  [the longest x2 3.57 us: body(): log_total[parent_rows]]
    reduce_sum x4 -> x0, other arithmetic: 3.42 us -> none  [the longest x1 1.85 us: body(): square = jnp.sum(stream * stream, axis=1)]
  transfers between devices with their start and end apart: 2 -> 0, of which waited for: 2 -> 0; matrix products, arithmetic and copies ran while one was open for 0% -> 0% of each run, Pallas kernels for 0% -> 0%
where the time goes in v3:
time: 135 us
  Pallas kernels  129 us (96%)
  between operations  3.63 us (3%)
  local copies, waits for them, and re-layouts  2.59 us (2%)
    pallas_call x1, Pallas kernels, whole(): pl.pallas_call(functools.partial(whole_kernel, scale * math.log2(math.e))...  129 us

profile of v3, /device:TPU:1, one launch (start us, length us, event | category | flops | bytes accessed | tf_op | source)
XLA Modules:
  0.0 135.2 jit_solution(7926547084206821895)
XLA Ops:
  1.9 129.0 %whole.1 = (bf16[64,448]{1,0:T(8,128)(2,1)}, f32[1,64]{1,0:T(1,128)}, f32[1,1]{1,0:T(1,128)}) custom-call(s32[1]{0:T(128)S(6)} %copy.22.len_ref, s32[1]{0:T(128)S(6)} %copy.23.accept_ref, bf16[64,8,128]{2,1,0:T(8,128)(2,1)} %bitcast.11, bf16[64,8,64]{2,1,0:T(8,128)(2,1)} %bitcast.12, bf16[8,128,512]{2,1,0:T(8,128)(2,1)} %ak_ref.1, ...), custom_call_target="tpu_custom_call" | custom-call | tf_op jit(solution)/shard_map/whole/pallas_call | solution.py:528
  130.9 1.5 %copy.24 = bf16[64,448]{1,0:T(8,128)(2,1)} copy(bf16[64,448]{1,0:T(8,128)(2,1)} %get-tuple-element.12) | data formatting | bytes 114688
  132.4 1.1 copy.25

commit v4 on v3

--- a/solution.py
+++ b/solution.py
@@ -20,10 +20,11 @@
 TRANS_B = (((1,), (1,)), ((), ()))
 
 
-def whole_kernel(scale, len_ref, accept_ref, nope_ref, rope_ref, ak_ref, kl_ref, kr_ref, dl_ref, dr_ref, parent_ref, ids_ref,
-                 av_ref, proj_ref, resid_ref, gain_ref, lm_ref, hid_ref, target_ref, score_ref,
+def whole_kernel(scale, len_ref, accept_ref, nope_hbm, rope_hbm, ak_hbm, kl_ref, kr_ref, dl_hbm, dr_hbm, parent_ref, ids_ref,
+                 av_ref, proj_ref, resid_hbm, gain_hbm, lm_ref, hid_ref, target_ref, score_ref,
                  qbuf, kbuf, krbuf, avbuf, acc, top, mass, part, part_in, stat, stat_in, lse, tree, names, rows_ref,
                  proj, lm, out_part, out_in, near, near_in, padded, hid_own, hid_in, wide, logits, rates, tiles, merged, tile1, tile2,
+                 nope_ref, rope_ref, ak_ref, dl_ref, dr_ref, resid_ref, gain_ref,
                  loc_sem, q_send, q_recv, k_send, k_recv, r_send, r_recv, v_send, v_recv, p_send, p_recv,
                  s_send, s_recv, n_sem, h_sem, g1_send, g1_recv, g2_send, g2_recv, g3_send, g3_recv,
                  c_send, c_recv, f1_send, f1_recv, f2_send, f2_recv):
@@ -68,6 +69,9 @@
         return copy
 
     local = []
+    nope_in = [local_copy(nope_hbm, nope_ref, 7), local_copy(rope_hbm, rope_ref, 8), local_copy(ak_hbm, ak_ref, 9)]
+    small_in = [local_copy(dl_hbm, dl_ref, 10), local_copy(dr_hbm, dr_ref, 11)]
+    late_in = [local_copy(resid_hbm, resid_ref, 12), local_copy(gain_hbm, gain_ref, 13)]
     for h in range(2):
         local.append(local_copy(kl_ref.at[pl.ds(512 * h, 512)], kbuf.at[h], h))
         local.append(local_copy(kr_ref.at[:, pl.ds(512 * h, 512)], krbuf.at[h, pl.ds(0, 64)], 2 + h))
@@ -79,12 +83,16 @@
     half = lambda h: pl.ds(256 * h, 256)
     sends = []
     q_in, k_in, r_in = {}, {}, {}
-    for slot, peer, order in ((1, z_right, (0, 1)), (2, z_left, (1, 0))):
-        for h in order:
-            n = slot * 2 + h
-            k_in[n] = remote(kl_ref.at[pl.ds(512 * h, 512)], kbuf.at[n], k_send.at[n], k_recv.at[n], peer)
-            r_in[n] = remote(kr_ref.at[:, pl.ds(512 * h, 512)], krbuf.at[n, pl.ds(0, 64)], r_send.at[n], r_recv.at[n], peer)
-
+    def key_send(slot, h, peer):
+        n = slot * 2 + h
+        k_in[n] = remote(kl_ref.at[pl.ds(512 * h, 512)], kbuf.at[n], k_send.at[n], k_recv.at[n], peer)
+        r_in[n] = remote(kr_ref.at[:, pl.ds(512 * h, 512)], krbuf.at[n, pl.ds(0, 64)], r_send.at[n], r_recv.at[n], peer)
+
+    key_send(1, 0, z_right)
+    key_send(2, 1, z_left)
+
+    for copy in nope_in:
+        copy.wait()
     content = jnp.swapaxes(nope_ref[...].astype(f32), 0, 1).astype(bf)
     rotary = jnp.swapaxes(rope_ref[...].astype(f32), 0, 1).astype(bf)
     for h in range(8):
@@ -109,6 +117,8 @@
     own_parents = jnp.sum(jnp.where(own_line, names[0:8], 0.0), axis=0, keepdims=True)
     own_parents = jnp.transpose(jnp.broadcast_to(own_parents, (128, 128))).astype(jnp.int32)
     tree[...] = jnp.zeros_like(tree)
+    for copy in small_in:
+        copy.wait()
     tree[0:64, 0:512] = dl_ref[...]
     tree[0:64, 512:576] = dr_ref[...]
     for n in range(8):
@@ -171,26 +181,6 @@
     q_in[6] = remote(qbuf.at[1, half(0)], qbuf.at[3, half(0)], q_send.at[6], q_recv.at[6], y_right)
     q_in[5].wait_recv()
     q_in[7] = remote(qbuf.at[2, half(1)], qbuf.at[3, half(1)], q_send.at[7], q_recv.at[7], y_left)
-    q_in[3].wait_recv()
-    q_in[4].wait_recv()
-    chunks(0, 2, (1, 2))
-
-    def key_wait(n):
-        k_in[n].wait_recv()
-        r_in[n].wait_recv()
-
-    def key_on(n, m, peer):
-        k_in[m] = remote(kbuf.at[n], kbuf.at[m], k_send.at[m], k_recv.at[m], peer)
-        r_in[m] = remote(krbuf.at[n, pl.ds(0, 64)], krbuf.at[m, pl.ds(0, 64)], r_send.at[m], r_recv.at[m], peer)
-
-    key_wait(2)
-    key_on(2, 6, z_right)
-    key_wait(5)
-    key_on(5, 7, z_left)
-    chunks(2, 1, (0, 1, 2))
-    chunks(5, 1, (0, 1, 2))
-    q_in[6].wait_recv()
-    q_in[7].wait_recv()
     v_in = {}
     mine = 4 * c
     pair = lambda first, h: pl.ds(first + 2 * h, 2)
@@ -198,28 +188,56 @@
         for h in order:
             n = slot * 2 + h
             v_in[n] = remote(av_ref.at[pair(mine, h)], avbuf.at[slot, pair(mine, h)], v_send.at[n], v_recv.at[n], peer)
+
+    def key_wait(n):
+        k_in[n].wait_recv()
+        r_in[n].wait_recv()
+
+    def key_on(n, m, peer):
+        k_in[m] = remote(kbuf.at[n], kbuf.at[m], k_send.at[m], k_recv.at[m], peer)
+        r_in[m] = remote(krbuf.at[n, pl.ds(0, 64)], krbuf.at[m, pl.ds(0, 64)], r_send.at[m], r_recv.at[m], peer)
+
+    key_wait(2)
+    key_on(2, 6, z_right)
+    key_wait(5)
+    key_on(5, 7, z_left)
+    q_in[3].wait_recv()
+    q_in[4].wait_recv()
+    chunks(0, 2, (1, 2))
+    chunks(2, 1, (0, 1, 2))
+    chunks(5, 1, (0, 1, 2))
+    q_in[6].wait_recv()
+    q_in[7].wait_recv()
     chunks(0, 3, (3,))
     chunks(5, 1, (3,))
+    for n in (6, 7):
+        k_in[n].wait_send()
+        r_in[n].wait_send()
+    key_send(1, 1, z_right)
+    key_send(2, 0, z_left)
     v_in[2].wait_recv()
     v_in[6] = remote(avbuf.at[1, pair(mine, 0)], avbuf.at[3, pair(mine, 0)], v_send.at[6], v_recv.at[6], y_right)
     v_in[5].wait_recv()
     v_in[7] = remote(avbuf.at[2, pair(mine, 1)], avbuf.at[3, pair(mine, 1)], v_send.at[7], v_recv.at[7], y_left)
-    key_wait(3)
-    key_wait(4)
-    chunks(3, 2, (0, 1, 2, 3))
+    key_wait(6)
+    key_wait(7)
+    chunks(6, 2, (0, 1, 2, 3))
     v_in[3].wait_recv()
     v_in[4].wait_recv()
     v_over = {}
-    for slot in (1, 2):
-        v_over[slot] = remote(avbuf.at[slot, pl.ds(mine, 4)], avbuf.at[slot, pl.ds(mine, 4)], v_send.at[7 + slot], v_recv.at[7 + slot], sibling)
+
+    def heads_over(slot):
+        some = avbuf.at[slot, pl.ds(mine, 4)]
+        v_over[slot] = remote(some, some, v_send.at[7 + slot], v_recv.at[7 + slot], sibling)
+
+    heads_over(1)
+    heads_over(2)
     v_in[6].wait_recv()
     v_in[7].wait_recv()
-    v_over[3] = remote(avbuf.at[3, pl.ds(mine, 4)], avbuf.at[3, pl.ds(mine, 4)], v_send.at[10], v_recv.at[10], sibling)
-    key_wait(6)
-    key_wait(7)
+    heads_over(3)
+    key_wait(3)
+    key_wait(4)
     local_av.wait()
-    for slot in (1, 2, 3):
-        v_over[slot].wait_recv()
 
     def finish(slot):
         for h in range(8):
@@ -234,12 +252,13 @@
             stat[slot, pl.ds(k, 1)] = jnp.transpose(lse[pl.ds(128 * k, 128)])[:1]
 
     p_in = []
-    for slot, landing, peer in ((3, 3, y_far), (1, 2, y_left), (2, 1, y_right)):
-        chunks(6, 2, (slot,))
+    for slot, landing, peer in ((1, 2, y_left), (2, 1, y_right), (3, 3, y_far)):
+        chunks(3, 2, (slot,))
+        v_over[slot].wait_recv()
         finish(slot)
         p_in.append(remote(part.at[slot], part_in.at[landing], p_send.at[landing], p_recv.at[landing], peer))
         p_in.append(remote(stat.at[slot], stat_in.at[landing], p_send.at[landing + 4], p_recv.at[landing + 4], peer))
-    chunks(6, 2, (0,))
+    chunks(3, 2, (0,))
     finish(0)
     for copy in p_in:
         copy.wait_recv()
@@ -273,6 +292,8 @@
         out_part[2 * g + 1] = block[32:]
 
     proj_copy.wait()
+    for copy in late_in:
+        copy.wait()
     make(lax.rem(group + 1, 8))
 
     def spread(k, _):
@@ -347,41 +368,44 @@
 
     pending = []
     hid_own[...] = stream.astype(bf)
-    hid_copy = None
-    waits = {}
-    for stage, (sends, recvs) in enumerate(((g1_send, g1_recv), (g2_send, g2_recv))):
-        for p in range(3):
-            axis, done = orders[p][stage], orders[p][:stage]
-            for k in (1, 3, 2):
-                n = p * 3 + k - 1
-                own = view(p, done, here)
-                copy = remote(own, own, sends.at[n], recvs.at[n], turned(axis, k))
-                pending.append(copy)
-                waits[stage, p, k] = (done, axis, n, sends, recvs)
-        if stage == 0:
-            hid_copy = remote(hid_own, hid_in.at[zl], h_sem.at[0], h_sem.at[1], partner)
-            hid_in[zl] = hid_own[...]
-        for p in range(3):
-            done, axis = orders[p][:stage], orders[p][stage]
-            for k in (1, 3, 2):
-                n = p * 3 + k - 1
-                came = view(p, done, moved(axis, 4 - k))
-                describe(came, came, sends.at[n], recvs.at[n], turned(axis, k)).wait_recv()
+    stages = ((g1_send, g1_recv), (g2_send, g2_recv))
+
+    def begin(stage, p):
+        sends, recvs = stages[stage]
+        for k in (1, 3, 2):
+            n = p * 3 + k - 1
+            own = view(p, orders[p][:stage], here)
+            pending.append(remote(own, own, sends.at[n], recvs.at[n], turned(orders[p][stage], k)))
+
+    def await_stage(stage, p):
+        sends, recvs = stages[stage]
+        axis = orders[p][stage]
+        for k in (1, 3, 2):
+            n = p * 3 + k - 1
+            came = view(p, orders[p][:stage], moved(axis, 4 - k))
+            describe(came, came, sends.at[n], recvs.at[n], turned(axis, k)).wait_recv()
+
     sibling = {"batch_1": 1 - c}
 
     def over(p, n, which):
-        copy = remote(which, which, c_send.at[n], c_recv.at[n], sibling)
-        pending.append(copy)
+        pending.append(remote(which, which, c_send.at[n], c_recv.at[n], sibling))
 
     for p in range(3):
+        begin(0, p)
+    hid_copy = remote(hid_own, hid_in.at[zl], h_sem.at[0], h_sem.at[1], partner)
+    hid_in[zl] = hid_own[...]
+    for p in range(3):
+        await_stage(0, p)
+        begin(1, p)
+    for p in range(3):
+        await_stage(1, p)
         axis, done = orders[p][2], orders[p][:2]
         for k, halves in ((1, (0, 1)), (3, (1, 0))):
             for half in halves:
                 n = p * 6 + (k // 2) * 2 + half
                 own = view(p, done, here, half)
                 pending.append(remote(own, own, g3_send.at[n], g3_recv.at[n], turned(axis, k)))
-    for p in range(3):
-        over(p, p * 4, view(p, orders[p][:2], here))
+        over(p, p * 4, view(p, done, here))
 
     def came3(p, k, half):
         axis, done = orders[p][2], orders[p][:2]
@@ -514,6 +538,8 @@
     lax.fori_loop(1, 15, sent, 0)
     for copy in pending:
         copy.wait_send()
+    for n in (6, 7):
+        del k_in[n], r_in[n]
     for table in (q_in, k_in, r_in, v_in, v_over):
         for copy in table.values():
             copy.wait_send()
@@ -532,7 +558,7 @@
             jax.ShapeDtypeStruct((1, 64), f32),
             jax.ShapeDtypeStruct((1, 1), f32),
         ),
-        in_specs=[sm, sm, vm, vm, vm, hbm, hbm, vm, vm, vm, vm, hbm, hbm, vm, vm, hbm],
+        in_specs=[sm, sm, hbm, hbm, hbm, hbm, hbm, hbm, hbm, vm, vm, hbm, hbm, hbm, hbm, hbm],
         out_specs=(vm, vm, vm),
         scratch_shapes=[
             vmem((4, 512, 640), bf), vmem((8, 512, 512), bf), vmem((8, 128, 512), bf), vmem((4, 8, 512, 128), bf),
@@ -544,7 +570,9 @@
             vmem((4, 2, 4, 2, 2, 32, 1024), bf),
             vmem((4, 2, 64, 512), f32), vmem((4, 2, 64, 128), f32), vmem((8, 8, 128), f32), vmem((8, 128), f32),
             vmem((8, 8, 128), f32), vmem((16, 8, 128), f32),
-            dma((7,)), dma((8,)), dma((8,)), dma((8,)), dma((8,)), dma((8,)), dma((8,)),
+            vmem((64, 8, 128), bf), vmem((64, 8, 64), bf), vmem((8, 128, 512), bf), vmem((64, 512), bf), vmem((64, 64), bf),
+            vmem((64, 448), bf), vmem((1, 7168), f32),
+            dma((14,)), dma((8,)), dma((8,)), dma((8,)), dma((8,)), dma((8,)), dma((8,)),
             dma((11,)), dma((11,)), dma((8,)), dma((8,)),
             dma((16,)), dma((16,)), dma((2,)), dma((2,)), dma((9,)), dma((9,)), dma((9,)), dma((9,)),
             dma((18,)), dma((18,)), dma((12,)), dma((12,)), dma((8,)), dma((8,)), dma((16,)), dma((16,)),

time: 135 us -> 130 us (0.963)
  Pallas kernels: 129 us -> 123 us
    pallas_call x1, Pallas kernels: 129 us -> 123 us  [whole(): pl.pallas_call(functools.partial(whole_kernel, scale * math.log2(math.e))...]
where the time goes in v4:
time: 130 us
  Pallas kernels  123 us (95%)
  between operations  3.63 us (3%)
  local copies, waits for them, and re-layouts  2.59 us (2%)
    pallas_call x1, Pallas kernels, whole(): pl.pallas_call(functools.partial(whole_kernel, scale * math.log2(math.e))...  123 us

profile of v4, /device:TPU:1, one launch (start us, length us, event | category | flops | bytes accessed | tf_op | source)
XLA Modules:
  0.0 129.6 jit_solution(16895806632788499717)
XLA Ops:
  1.9 123.4 %whole.1 = (bf16[64,448]{1,0:T(8,128)(2,1)}, f32[1,64]{1,0:T(1,128)}, f32[1,1]{1,0:T(1,128)}) custom-call(s32[1]{0:T(128)S(6)} %copy.22.len_ref, s32[1]{0:T(128)S(6)} %copy.23.accept_ref, bf16[64,8,128]{2,1,0:T(8,128)(2,1)} %bitcast.11, bf16[64,8,64]{2,1,0:T(8,128)(2,1)} %bitcast.12, bf16[8,128,512]{2,1,0:T(8,128)(2,1)} %ak_hbm.1, ...), custom_call_target="tpu_custom_call" | custom-call | tf_op jit(solution)/shard_map/whole/pallas_call | solution.py:554
  125.3 1.5 %copy.24 = bf16[64,448]{1,0:T(8,128)(2,1)} copy(bf16[64,448]{1,0:T(8,128)(2,1)} %get-tuple-element.12) | data formatting | bytes 114688
  126.8 1.1 copy.25

commit v5 on v4

--- a/solution.py
+++ b/solution.py
@@ -253,7 +253,8 @@
 
     p_in = []
     for slot, landing, peer in ((1, 2, y_left), (2, 1, y_right), (3, 3, y_far)):
-        chunks(3, 2, (slot,))
+        if slot != 2:
+            chunks(3, 2, (1, 2) if slot == 1 else (slot,))
         v_over[slot].wait_recv()
         finish(slot)
         p_in.append(remote(part.at[slot], part_in.at[landing], p_send.at[landing], p_recv.at[landing], peer))
@@ -447,26 +448,19 @@
         rate = lax.rsqrt(jnp.sum(squares, axis=1, keepdims=True) * (1.0 / (64 * 7168)) + norm_epsilon)
         rates[:, core] = jnp.broadcast_to(rate, (256, 128)).reshape(4, 64, 128)
 
-    contract(c)
-    for p in range(3):
-        axis, done = orders[p][2], orders[p][:2]
-        for n, by in ((0, 0), (1, 3), (2, 1), (3, 2)):
-            block = view(p, done, {**moved(axis, by), "c": 1 - c})
-            describe(block, block, c_send.at[p * 4 + n], c_recv.at[p * 4 + n], sibling).wait_recv()
-    contract(1 - c)
     vocab_first = (me * 8 + place) * 512
     entry = lax.broadcasted_iota(jnp.int32, (64, 512), 1) + vocab_first
     spot = lax.broadcasted_iota(jnp.int32, (64, 128), 1)
     tiles[...] = jnp.zeros_like(tiles)
 
     def column(r):
-        return jnp.transpose(jnp.broadcast_to(names[r : r + 1], (128, 128)))[:64].astype(jnp.int32)
-
-    for k in range(4):
-        found = [[], [], []]
-        for h in range(2):
-            parents, wanted = column(2 * k + h), column(8 + 2 * k + h)
-            values = logits[k, h] * jnp.tile(rates[k, h], (1, 4))
+        return jnp.transpose(jnp.broadcast_to(names[pl.ds(r, 1)], (128, 128)))[:64].astype(jnp.int32)
+
+    def summarise(core):
+        for k in range(4):
+            b = 2 * k + core
+            parents, wanted = column(b), column(8 + b)
+            values = logits[k, core] * jnp.tile(rates[k, core], (1, 4))
             best = jnp.max(values, axis=1, keepdims=True)
             mass_here = jnp.sum(jnp.exp(values - best), axis=1, keepdims=True)
             choose = (parents == spot).astype(bf)[:, :64]
@@ -478,11 +472,18 @@
             hit = entry == jnp.tile(wanted, (1, 4))
             pick = jnp.sum(jnp.where(hit, source, 0.0), axis=1, keepdims=True)
             for i, one in enumerate((best, mass_here, pick)):
-                found[i].append(jnp.broadcast_to(one, (64, 128)))
-        for i in range(3):
-            line = jnp.transpose(jnp.concatenate(found[i], axis=0))[:8]
-            tiles[2 * k, i : i + 1] = line[:1]
-            tiles[2 * k + 1, i : i + 1] = pltpu.roll(line, 64, 1)[:1]
+                square = jnp.concatenate([jnp.broadcast_to(one, (64, 128)), jnp.zeros((64, 128), f32)], axis=0)
+                tiles[b, i : i + 1] = jnp.transpose(square)[:1]
+
+    contract(c)
+    summarise(c)
+    for p in range(3):
+        axis, done = orders[p][2], orders[p][:2]
+        for n, by in ((0, 0), (1, 3), (2, 1), (3, 2)):
+            block = view(p, done, {**moved(axis, by), "c": 1 - c})
+            describe(block, block, c_send.at[p * 4 + n], c_recv.at[p * 4 + n], sibling).wait_recv()
+    contract(1 - c)
+    summarise(1 - c)
 
     def merge(blocks):
         best = functools.reduce(jnp.maximum, [b[0:1] for b in blocks])

time: 130 us -> 129 us (level)
  no operation moved by 1% of the time
where the time goes in v5:
time: 129 us
  Pallas kernels  123 us (95%)
  between operations  3.63 us (3%)
  local copies, waits for them, and re-layouts  2.59 us (2%)
    pallas_call x1, Pallas kernels, whole(): pl.pallas_call(functools.partial(whole_kernel, scale * math.log2(math.e))...  123 us
    unnamed x2, local copies, waits for them, and re-layouts  2.59 us

profile of v5, /device:TPU:1, one launch (start us, length us, event | category | flops | bytes accessed | tf_op | source)
XLA Modules:
  0.0 128.8 jit_solution(12761506734112648191)
XLA Ops:
  1.9 122.6 %whole.1 = (bf16[64,448]{1,0:T(8,128)(2,1)}, f32[1,64]{1,0:T(1,128)}, f32[1,1]{1,0:T(1,128)}) custom-call(s32[1]{0:T(128)S(6)} %copy.22.len_ref, s32[1]{0:T(128)S(6)} %copy.23.accept_ref, bf16[64,8,128]{2,1,0:T(8,128)(2,1)} %bitcast.11, bf16[64,8,64]{2,1,0:T(8,128)(2,1)} %bitcast.12, bf16[8,128,512]{2,1,0:T(8,128)(2,1)} %ak_hbm.1, ...), custom_call_target="tpu_custom_call" | custom-call | tf_op jit(solution)/shard_map/whole/pallas_call | solution.py:555
  124.5 1.5 %copy.24 = bf16[64,448]{1,0:T(8,128)(2,1)} copy(bf16[64,448]{1,0:T(8,128)(2,1)} %get-tuple-element.12) | data formatting | bytes 114688
  126.0 1.1 copy.25
